TPU v7x, 512 devices: a whole 4x4x16 slice. The times are simulated.
512 devices in a mesh: gx: 16 (over z_lo, x), yz: 32 (over z_hi, y, core).
Axes of the slice: x: 4, y: 4, z: 16 (z_hi: 4, z_lo: 4; z = z_hi * 4 + z_lo), core: 2. Of those that a mesh axis runs over, the one named last changes fastest.
Arguments:
- nodes: float32 [3, 2097152], P(None, ('gx', 'yz')), may hold values from -4 to 4
- links: int32 [2, 2097152], P(None, ('gx', 'yz')), may hold values from 0 to 4095, as said below
- burgers: float32 [3, 2097152], P(None, ('gx', 'yz')), may hold values from -4 to 4
- mobility: float32 [3, 3, 2097152], P(None, None, ('gx', 'yz'))
- send_list: int32 [512, 8, 6], P(('gx', 'yz')), may hold values from 0 to 31
- pair_list: int32 [2, 81920], P(None, ('gx', 'yz')), may hold values from 0 to 79, as said below
- pair_count: int32 [512], P(('gx', 'yz')), may hold values from 48 to 160, as said below
Outputs:
- displacement: float32 [3, 2097152], P(None, ('gx', 'yz'))
Inputs may be any that keep to these rules, and one draw needn't show every extreme that they name: Within each domain the links form one closed loop: every node of the domain ends exactly two of its segments; entries are node numbers within the domain. `pair_list`: row 0 holds target block numbers below 32; row 1 holds source numbers; every ghost slot of a domain is named by one of its live entries; entries at or past the domain's pair_count are unused. `pair_count`: the largest count equals 160 in every draw.
All inputs are finite; a program needn't handle non-finite values.
Results may differ from a plain program's by a relative error of at most 0.0003.
Values sent between devices are 32-bit elements; how exact they have to be, the bound alone decides.
A program may use at most 64 MiB of HBM per device.

v0:
```python
import jax
import jax.numpy as jnp
from jax import lax
from jax.sharding import PartitionSpec as P

A_SQUARED = 0.25
NU_FACTOR = 0.4
DX_LIMIT = 1.0
SPEED_EPS = 1e-05
DIRECTIONS = ((-1, -1), (-1, 0), (-1, 1), (0, -1), (0, 1), (1, -1), (1, 0), (1, 1))


def shifted(value, axis, steps):
    count = lax.axis_size(axis)
    pairs = [(source, (source + steps) % count) for source in range(count)]
    return lax.ppermute(value, axis, pairs)


def crossed(left, right):
    return jnp.stack(
        [
            left[1] * right[2] - left[2] * right[1],
            left[2] * right[0] - left[0] * right[2],
            left[0] * right[1] - left[1] * right[0],
        ]
    )


def make_blocks(points, links, burgers):
    first = jnp.take(points, links[0], axis=1)
    second = jnp.take(points, links[1], axis=1)
    data = jnp.concatenate([0.5 * (first + second), second - first, burgers], axis=0)
    return data.reshape(9, -1, 128).transpose(1, 0, 2)


def tile_traction(target, source):
    relative = target[0:3, :, None] - source[0:3, None, :]
    distance = jnp.sum(relative * relative, axis=0) + A_SQUARED
    inv_cube = 1.0 / (distance * jnp.sqrt(distance))
    line_src = source[3:6, None, :]
    burg_src = source[6:9, None, :]
    burg_tgt = target[6:9, :, None]
    across = crossed(burg_src, relative)
    twisted = jnp.sum(burg_src * crossed(line_src, relative), axis=0)
    along = jnp.sum(across * burg_tgt, axis=0)
    lined = jnp.sum(line_src * burg_tgt, axis=0)
    weight_line = 0.5 * inv_cube * along
    weight_cross = 0.5 * inv_cube * lined
    weight_self = NU_FACTOR * inv_cube * twisted
    return (
        jnp.sum(weight_line[None] * line_src, axis=2)
        + jnp.sum(weight_cross[None] * across, axis=2)
        + burg_tgt[:, :, 0] * jnp.sum(weight_self, axis=1)[None]
    )


def traction_sum(blocks, sources, pair_rows, live_count):

    def group_step(group_index, running):
        chosen = lax.dynamic_slice_in_dim(pair_rows, group_index * 8, 8, 1)
        tile_terms = jax.vmap(tile_traction)(blocks[chosen[0]], sources[chosen[1]])
        live_mask = group_index * 8 + jnp.arange(8) < live_count
        tile_terms = jnp.where(live_mask[:, None, None], tile_terms, 0.0)
        return running.at[chosen[0]].add(tile_terms)

    start_value = jnp.zeros((blocks.shape[0], 3, blocks.shape[2]), jnp.float32)
    return lax.fori_loop(0, pair_rows.shape[1] // 8, group_step, start_value)


def nodal_velocity(traction, blocks, links, mobility):
    seg_count = links.shape[1]
    traction_rows = traction.transpose(1, 0, 2).reshape(3, seg_count)
    line_rows = blocks[:, 3:6].transpose(1, 0, 2).reshape(3, seg_count)
    half_force = 0.5 * crossed(traction_rows, line_rows)
    nodal = jnp.zeros((3, mobility.shape[2]), jnp.float32)
    nodal = nodal.at[:, links[0]].add(half_force).at[:, links[1]].add(half_force)
    return jnp.sum(mobility * nodal[None], axis=1)


def gather_ghosts(outgoing):
    arrivals = []
    for place, item in enumerate(DIRECTIONS):
        moving = outgoing[place]
        if item[1] != 0:
            moving = shifted(moving, "yz", item[1])
        if item[0] != 0:
            moving = shifted(moving, "gx", item[0])
        arrivals.append(moving)
    stacked = jnp.stack(arrivals)
    return stacked.reshape(-1, 9, stacked.shape[-1])


def velocity_at(points, links, burgers, mobility, send_list, pair_list, pair_count):
    blocks = make_blocks(points, links, burgers)
    outgoing = blocks[send_list[0]]
    sources = jnp.concatenate([blocks, gather_ghosts(outgoing)], axis=0)
    traction = traction_sum(blocks, sources, pair_list, pair_count[0])
    return nodal_velocity(traction, blocks, links, mobility)


def local(nodes, links, burgers, mobility, send_list, pair_list, pair_count):
    first_speed = velocity_at(nodes, links, burgers, mobility, send_list, pair_list, pair_count)
    local_top = jnp.max(jnp.sqrt(jnp.sum(first_speed * first_speed, axis=0)))
    global_top = lax.pmax(local_top, ("gx", "yz"))
    step_size = DX_LIMIT / (global_top + SPEED_EPS)
    moved = nodes + step_size * first_speed
    second_speed = velocity_at(moved, links, burgers, mobility, send_list, pair_list, pair_count)
    return 0.5 * step_size * (first_speed + second_speed)


def solution(mesh):
    return jax.shard_map(
        local,
        mesh=mesh,
        in_specs=(
            P(None, ("gx", "yz")),
            P(None, ("gx", "yz")),
            P(None, ("gx", "yz")),
            P(None, None, ("gx", "yz")),
            P(("gx", "yz"), None, None),
            P(None, ("gx", "yz")),
            P(("gx", "yz")),
        ),
        out_specs=P(None, ("gx", "yz")),
        check_vma=False,
    )
```

profile of v0, /device:TPU:1, one launch (start us, length us, event | category | flops | bytes accessed | tf_op | source)
XLA Modules:
  0.0 665.4 jit_solution(3275787010613865413)
XLA Ops:
  0.9 1.5 copy.249
  2.4 14.1 %gather_fusion.6 = f32[4096,3]{1,0:T(8,128)} fusion(f32[3,4096]{0,1:T(8,128)S(1)} %copy.249, s32[4096]{0:T(1024)S(1)} %get-tuple-element.432), kind=kCustom, calls=%fused_computation.clone | custom fusion | bytes 114688 | tf_op jit(solution)/shard_map/jit(_take)/gather | solution.py:30
  16.5 2.2 copy.250
  18.7 14.1 %gather_fusion.7 = f32[4096,3]{1,0:T(8,128)} fusion(f32[3,4096]{0,1:T(8,128)S(1)} %copy.249, s32[4096]{0:T(1024)S(1)} %get-tuple-element.433), kind=kCustom, calls=%fused_computation.5.clone | custom fusion | bytes 114688 | tf_op jit(solution)/shard_map/jit(_take)/gather | solution.py:31
  32.8 2.2 copy.252
  36.5 8.8 %collective-permute-start = (f32[6,9,128]{2,1,0:T(8,128)S(1)}, f32[6,9,128]{2,1,0:T(8,128)S(1)}, u32[]{:S(2)}, u32[]{:S(2)}) collective-permute-start(f32[6,9,128]{2,1,0:T(8,128)S(1)} %get-tuple-element.413), channel_id=1, source_target_pairs={{0,31},{1,0},{2,1},{3,2},{4,3},{5,4},{6,5},{7,6},{8,7},{9,8},{10,9... | collective-permute-start | bytes 82952 | tf_op jit(solution)/shard_map/ppermute | solution.py:16
  45.3 3.1 collective-permute-start.2
  48.4 3.4 collective-permute-start.3
  51.8 10.7 %collective-permute-start.5 = (f32[6,9,128]{2,1,0:T(8,128)S(1)}, f32[6,9,128]{2,1,0:T(8,128)S(1)}, u32[]{:S(2)}, u32[]{:S(2)}) collective-permute-start(f32[6,9,128]{2,1,0:T(8,128)S(1)} %get-tuple-element.410), channel_id=1, source_target_pairs={{0,31},{1,0},{2,1},{3,2},{4,3},{5,4},{6,5},{7,6},{8,7},{9,8},{10,9... | collective-permute-start | bytes 82952 | tf_op jit(solution)/shard_map/ppermute | solution.py:16
  62.5 1.9 collective-permute-start.6
  64.5 2.5 collective-permute-start.1
  67.0 2.6 collective-permute-done.1
  69.7 10.5 %collective-permute-start.7 = (f32[6,9,128]{2,1,0:T(8,128)S(1)}, f32[6,9,128]{2,1,0:T(8,128)S(1)}, u32[]{:S(2)}, u32[]{:S(2)}) collective-permute-start(f32[6,9,128]{2,1,0:T(8,128)S(1)} %get-tuple-element.408), channel_id=1, source_target_pairs={{0,31},{1,0},{2,1},{3,2},{4,3},{5,4},{6,5},{7,6},{8,7},{9,8},{10,9... | collective-permute-start | bytes 82952 | tf_op jit(solution)/shard_map/ppermute | solution.py:16
  80.2 1.9 collective-permute-start.10
  82.1 6.4 collective-permute-start.4
  88.5 1.9 collective-permute-start.9
  90.5 1.9 collective-permute-start.8
  92.4 1.9 collective-permute-start.11
  94.4 4.8 collective-permute-done.8
  99.3 1.9 collective-permute-done.11
  101.5 133.7 %while.26 = (s32[]{:T(128)}, f32[32,3,128]{2,1,0:T(4,128)S(1)}, s32[2,160]{1,0:T(2,128)S(1)}, s32[]{:T(128)}, f32[32,9,128]{2,1,0:T(8,128)S(1)}, /*index=5*/f32[...) while((s32[]{:T(128)}, f32[32,3,128]{2,1,0:T(4,128)S(1)}, s32[2,160]{1,0:T(2,128)S(1)}, ...), condition=%wide.region_9.11_spmd, body=%wide.region_0.10_spmd.sunk | while | flops 10233926 | bytes 16958032 | solution.py:67
  104.8 1.1 multiply_reduce_fusion.28
  111.5 1.1 multiply_reduce_fusion.28
  118.2 1.1 multiply_reduce_fusion.28
  124.9 1.1 multiply_reduce_fusion.28
  131.6 1.1 multiply_reduce_fusion.28
  138.3 1.1 multiply_reduce_fusion.28
  144.9 1.1 multiply_reduce_fusion.28
  151.6 1.1 multiply_reduce_fusion.28
  158.3 1.1 multiply_reduce_fusion.28
  185.0 1.1 multiply_reduce_fusion.28
  191.7 1.1 multiply_reduce_fusion.28
  225.1 1.1 multiply_reduce_fusion.28
  235.3 2.0 copy.258
  237.3 23.2 %scatter_custom_fusion.2 = f32[3,4096]{0,1:T(8,128)S(1)} fusion(s32[4096]{0:T(1024)S(1)} %bitcast.301, f32[4096,3]{1,0:T(8,128)} %copy.258, f32[]{:T(128)} %constant.166.clone.1), kind=kCustom, calls=%fused_computation.92 | custom fusion | flops 12288 | bytes 49664 | tf_op jit(solution)/shard_map/scatter-add | solution.py:76
  260.5 23.4 %scatter_fusion.2 = f32[3,4096]{0,1:T(8,128)S(1)} fusion(f32[3,4096]{0,1:T(8,128)S(1)} %scatter_custom_fusion.2, s32[4096]{0:T(1024)S(1)} %bitcast.295, f32[4096,3]{1,0:T(8,128)} %copy.258), kind=kCustom, calls=%fused_computation.13 | custom fusion | flops 12288 | bytes 163840 | tf_op jit(solution)/shard_map/scatter-add | solution.py:76
  285.4 109.1 %pmax.7 = f32[]{:T(128)} all-reduce(f32[]{:T(128)} %sqrt_reduce_fusion), channel_id=1, replica_groups=mesh['gx'=16,'yz'=32] {'gx','yz'}, use_global_device_ids=true, to_apply=%region_15.17 | all-reduce | flops 1 | bytes 8 | tf_op jit(solution)/shard_map/pmax | solution.py:104
  395.9 14.1 %gather_fusion.8 = f32[4096,3]{1,0:T(8,128)} fusion(f32[3,4096]{0,1:T(8,128)S(1)} %copy.261, s32[4096]{0:T(1024)S(1)} %get-tuple-element.432), kind=kCustom, calls=%fused_computation.6.clone | custom fusion | bytes 114688 | tf_op jit(solution)/shard_map/jit(_take)/gather | solution.py:30
  410.0 14.1 %gather_fusion.9 = f32[4096,3]{1,0:T(8,128)} fusion(f32[3,4096]{0,1:T(8,128)S(1)} %copy.261, s32[4096]{0:T(1024)S(1)} %get-tuple-element.433), kind=kCustom, calls=%fused_computation.7.clone | custom fusion | bytes 114688 | tf_op jit(solution)/shard_map/jit(_take)/gather | solution.py:31
  424.1 2.4 copy.262
  428.0 2.6 collective-permute-start.12
  430.6 2.8 collective-permute-done.12
  433.4 4.8 collective-permute-start.13
  438.2 1.9 collective-permute-start.14
  440.1 2.2 collective-permute-start.15
  442.3 4.5 collective-permute-start.17
  446.9 1.9 collective-permute-start.18
  448.8 10.7 %collective-permute-start.19 = (f32[6,9,128]{2,1,0:T(8,128)S(1)}, f32[6,9,128]{2,1,0:T(8,128)S(1)}, u32[]{:S(2)}, u32[]{:S(2)}) collective-permute-start(f32[6,9,128]{2,1,0:T(8,128)S(1)} %get-tuple-element.400), channel_id=1, source_target_pairs={{0,31},{1,0},{2,1},{3,2},{4,3},{5,4},{6,5},{7,6},{8,7},{9,8},{10,9... | collective-permute-start | bytes 82952 | tf_op jit(solution)/shard_map/ppermute | solution.py:16
  459.5 1.9 collective-permute-start.22
  461.5 1.9 collective-permute-start.16
  463.4 3.4 collective-permute-start.21
  466.8 3.1 collective-permute-done.22
  469.9 2.3 collective-permute-start.20
  472.2 1.9 collective-permute-start.23
  474.2 4.4 collective-permute-done.20
  478.7 2.5 collective-permute-done.23
  481.5 133.7 %while.27 = (s32[]{:T(128)}, f32[32,3,128]{2,1,0:T(4,128)S(1)}, s32[2,160]{1,0:T(2,128)S(1)}, s32[]{:T(128)}, f32[32,9,128]{2,1,0:T(8,128)S(1)}, /*index=5*/f32[...) while((s32[]{:T(128)}, f32[32,3,128]{2,1,0:T(4,128)S(1)}, s32[2,160]{1,0:T(2,128)S(1)}, ...), condition=%wide.region_25.27_spmd, body=%wide.region_16.26_spmd.sunk | while | flops 10233926 | bytes 16958032 | solution.py:67
  484.8 1.1 multiply_reduce_fusion.33
  504.9 1.1 multiply_reduce_fusion.33
  525.0 1.1 multiply_reduce_fusion.33
  571.8 1.1 multiply_reduce_fusion.33
  615.3 2.0 copy.269
  617.3 23.2 %scatter_custom_fusion.4 = f32[3,4096]{0,1:T(8,128)S(1)} fusion(s32[4096]{0:T(1024)S(1)} %bitcast.302, f32[4096,3]{1,0:T(8,128)} %copy.269, f32[]{:T(128)} %constant.166.clone.1), kind=kCustom, calls=%fused_computation.90 | custom fusion | flops 12288 | bytes 49664 | tf_op jit(solution)/shard_map/scatter-add | solution.py:76
  640.5 23.4 %scatter_fusion.3 = f32[3,4096]{0,1:T(8,128)S(1)} fusion(f32[3,4096]{0,1:T(8,128)S(1)} %scatter_custom_fusion.4, s32[4096]{0:T(1024)S(1)} %bitcast.296, f32[4096,3]{1,0:T(8,128)} %copy.269), kind=kCustom, calls=%fused_computation.15 | custom fusion | flops 12288 | bytes 163840 | tf_op jit(solution)/shard_map/scatter-add | solution.py:76
  (1077 shorter events, 251.7 us)
Async XLA Ops:
  18.7 16.4 %copy-start.3 = (f32[3,4096]{1,0:T(4,128)S(1)}, f32[3,4096]{1,0:T(4,128)}, u32[]{:S(2)}) copy-start(f32[3,4096]{1,0:T(4,128)} %param.15) | copy-start | bytes 147460
  35.0 0.7 copy-start.6
  35.1 29.3 %copy-start.4 = (s32[2,4096]{1,0:T(2,128)S(1)}, s32[2,4096]{1,0:T(2,128)}, u32[]{:S(2)}) copy-start(s32[2,4096]{1,0:T(2,128)} %param.14) | copy-start | bytes 98308
  36.5 28.0 %collective-permute-start = (f32[6,9,128]{2,1,0:T(8,128)S(1)}, f32[6,9,128]{2,1,0:T(8,128)S(1)}, u32[]{:S(2)}, u32[]{:S(2)}) collective-permute-start(f32[6,9,128]{2,1,0:T(8,128)S(1)} %get-tuple-element.413), channel_id=1, source_target_pairs={{0,31},{1,0},{2,1},{3,2},{4,3},{5,4},{6,5},{7,6},{8,7},{9,8},{10,9... | collective-permute-start | bytes 82952 | tf_op jit(solution)/shard_map/ppermute | solution.py:16
  45.3 34.9 %collective-permute-start.2 = (f32[6,9,128]{2,1,0:T(8,128)S(1)}, f32[6,9,128]{2,1,0:T(8,128)S(1)}, u32[]{:S(2)}, u32[]{:S(2)}) collective-permute-start(f32[6,9,128]{2,1,0:T(8,128)S(1)} %get-tuple-element.412), channel_id=1, source_target_pairs={{0,480},{32,0},{64,32},{96,64},{128,96},{160,128},{192,160},{224,1... | collective-permute-start | bytes 82952 | tf_op jit(solution)/shard_map/ppermute | solution.py:16
  48.4 33.7 %collective-permute-start.3 = (f32[6,9,128]{2,1,0:T(8,128)S(1)}, f32[6,9,128]{2,1,0:T(8,128)S(1)}, u32[]{:S(2)}, u32[]{:S(2)}) collective-permute-start(f32[6,9,128]{2,1,0:T(8,128)S(1)} %get-tuple-element.411), channel_id=1, source_target_pairs={{0,1},{1,2},{2,3},{3,4},{4,5},{5,6},{6,7},{7,8},{8,9},{9,10},{10,1... | collective-permute-start | bytes 82952 | tf_op jit(solution)/shard_map/ppermute | solution.py:16
  51.8 42.6 %collective-permute-start.5 = (f32[6,9,128]{2,1,0:T(8,128)S(1)}, f32[6,9,128]{2,1,0:T(8,128)S(1)}, u32[]{:S(2)}, u32[]{:S(2)}) collective-permute-start(f32[6,9,128]{2,1,0:T(8,128)S(1)} %get-tuple-element.410), channel_id=1, source_target_pairs={{0,31},{1,0},{2,1},{3,2},{4,3},{5,4},{6,5},{7,6},{8,7},{9,8},{10,9... | collective-permute-start | bytes 82952 | tf_op jit(solution)/shard_map/ppermute | solution.py:16
  62.5 31.9 %collective-permute-start.6 = (f32[6,9,128]{2,1,0:T(8,128)S(1)}, f32[6,9,128]{2,1,0:T(8,128)S(1)}, u32[]{:S(2)}, u32[]{:S(2)}) collective-permute-start(f32[6,9,128]{2,1,0:T(8,128)S(1)} %get-tuple-element.409), channel_id=1, source_target_pairs={{0,1},{1,2},{2,3},{3,4},{4,5},{5,6},{6,7},{7,8},{8,9},{9,10},{10,1... | collective-permute-start | bytes 82952 | tf_op jit(solution)/shard_map/ppermute | solution.py:16
  64.5 5.1 collective-permute-start.1
  69.7 18.9 %collective-permute-start.7 = (f32[6,9,128]{2,1,0:T(8,128)S(1)}, f32[6,9,128]{2,1,0:T(8,128)S(1)}, u32[]{:S(2)}, u32[]{:S(2)}) collective-permute-start(f32[6,9,128]{2,1,0:T(8,128)S(1)} %get-tuple-element.408), channel_id=1, source_target_pairs={{0,31},{1,0},{2,1},{3,2},{4,3},{5,4},{6,5},{7,6},{8,7},{9,8},{10,9... | collective-permute-start | bytes 82952 | tf_op jit(solution)/shard_map/ppermute | solution.py:16
  80.2 21.3 %copy-start.5 = (s32[2,160]{1,0:T(2,128)S(1)}, s32[2,160]{1,0:T(2,128)}, u32[]{:S(2)}) copy-start(s32[2,160]{1,0:T(2,128)} %param.18) | copy-start | bytes 3844
  80.2 10.3 %collective-permute-start.10 = (f32[6,9,128]{2,1,0:T(8,128)S(1)}, f32[6,9,128]{2,1,0:T(8,128)S(1)}, u32[]{:S(2)}, u32[]{:S(2)}) collective-permute-start(f32[6,9,128]{2,1,0:T(8,128)S(1)} %get-tuple-element.406), channel_id=1, source_target_pairs={{0,1},{1,2},{2,3},{3,4},{4,5},{5,6},{6,7},{7,8},{8,9},{9,10},{10,1... | collective-permute-start | bytes 82952 | tf_op jit(solution)/shard_map/ppermute | solution.py:16
  82.1 10.3 %collective-permute-start.4 = (f32[6,9,128]{2,1,0:T(8,128)S(1)}, f32[6,9,128]{2,1,0:T(8,128)S(1)}, u32[]{:S(2)}, u32[]{:S(2)}) collective-permute-start(f32[6,9,128]{2,1,0:T(8,128)S(1)} %collective-permute-done.3), channel_id=1, source_target_pairs={{0,480},{32,0},{64,32},{96,64},{128,96},{160,128},{192,160},{224,1... | collective-permute-start | bytes 82952 | tf_op jit(solution)/shard_map/ppermute | solution.py:16
  88.5 10.7 %collective-permute-start.9 = (f32[6,9,128]{2,1,0:T(8,128)S(1)}, f32[6,9,128]{2,1,0:T(8,128)S(1)}, u32[]{:S(2)}, u32[]{:S(2)}) collective-permute-start(f32[6,9,128]{2,1,0:T(8,128)S(1)} %get-tuple-element.407), channel_id=1, source_target_pairs={{0,32},{32,64},{64,96},{96,128},{128,160},{160,192},{192,224},{224... | collective-permute-start | bytes 82952 | tf_op jit(solution)/shard_map/ppermute | solution.py:16
  90.5 8.7 %collective-permute-start.8 = (f32[6,9,128]{2,1,0:T(8,128)S(1)}, f32[6,9,128]{2,1,0:T(8,128)S(1)}, u32[]{:S(2)}, u32[]{:S(2)}) collective-permute-start(f32[6,9,128]{2,1,0:T(8,128)S(1)} %collective-permute-done.7), channel_id=1, source_target_pairs={{0,32},{32,64},{64,96},{96,128},{128,160},{160,192},{192,224},{224... | collective-permute-start | bytes 82952 | tf_op jit(solution)/shard_map/ppermute | solution.py:16
  92.4 8.7 %collective-permute-start.11 = (f32[6,9,128]{2,1,0:T(8,128)S(1)}, f32[6,9,128]{2,1,0:T(8,128)S(1)}, u32[]{:S(2)}, u32[]{:S(2)}) collective-permute-start(f32[6,9,128]{2,1,0:T(8,128)S(1)} %collective-permute-done.10), channel_id=1, source_target_pairs={{0,32},{32,64},{64,96},{96,128},{128,160},{160,192},{192,224},{224... | collective-permute-start | bytes 82952 | tf_op jit(solution)/shard_map/ppermute | solution.py:16
  260.5 24.1 %copy-start.1 = (f32[3,3,4096]{2,1,0:T(4,128)S(1)}, f32[3,3,4096]{2,1,0:T(4,128)}, u32[]{:S(2)}) copy-start(f32[3,3,4096]{2,1,0:T(4,128)} %param.16) | copy-start | bytes 442372
  283.9 111.3 %copy-start.2 = (f32[3,4096]{1,0:T(4,128)S(1)}, f32[3,4096]{1,0:T(4,128)}, u32[]{:S(2)}) copy-start(f32[3,4096]{1,0:T(4,128)} %param.13) | copy-start | bytes 147460
  424.0 2.4 copy-start
  428.0 5.4 collective-permute-start.12
  433.4 15.4 %collective-permute-start.13 = (f32[6,9,128]{2,1,0:T(8,128)S(1)}, f32[6,9,128]{2,1,0:T(8,128)S(1)}, u32[]{:S(2)}, u32[]{:S(2)}) collective-permute-start(f32[6,9,128]{2,1,0:T(8,128)S(1)} %collective-permute-done.12), channel_id=1, source_target_pairs={{0,480},{32,0},{64,32},{96,64},{128,96},{160,128},{192,160},{224,1... | collective-permute-start | bytes 82952 | tf_op jit(solution)/shard_map/ppermute | solution.py:16
  438.2 21.3 %collective-permute-start.14 = (f32[6,9,128]{2,1,0:T(8,128)S(1)}, f32[6,9,128]{2,1,0:T(8,128)S(1)}, u32[]{:S(2)}, u32[]{:S(2)}) collective-permute-start(f32[6,9,128]{2,1,0:T(8,128)S(1)} %get-tuple-element.404), channel_id=1, source_target_pairs={{0,480},{32,0},{64,32},{96,64},{128,96},{160,128},{192,160},{224,1... | collective-permute-start | bytes 82952 | tf_op jit(solution)/shard_map/ppermute | solution.py:16
  440.1 21.3 %collective-permute-start.15 = (f32[6,9,128]{2,1,0:T(8,128)S(1)}, f32[6,9,128]{2,1,0:T(8,128)S(1)}, u32[]{:S(2)}, u32[]{:S(2)}) collective-permute-start(f32[6,9,128]{2,1,0:T(8,128)S(1)} %get-tuple-element.403), channel_id=1, source_target_pairs={{0,1},{1,2},{2,3},{3,4},{4,5},{5,6},{6,7},{7,8},{8,9},{9,10},{10,1... | collective-permute-start | bytes 82952 | tf_op jit(solution)/shard_map/ppermute | solution.py:16
  442.3 31.9 %collective-permute-start.17 = (f32[6,9,128]{2,1,0:T(8,128)S(1)}, f32[6,9,128]{2,1,0:T(8,128)S(1)}, u32[]{:S(2)}, u32[]{:S(2)}) collective-permute-start(f32[6,9,128]{2,1,0:T(8,128)S(1)} %get-tuple-element.402), channel_id=1, source_target_pairs={{0,31},{1,0},{2,1},{3,2},{4,3},{5,4},{6,5},{7,6},{8,7},{9,8},{10,9... | collective-permute-start | bytes 82952 | tf_op jit(solution)/shard_map/ppermute | solution.py:16
  446.9 27.3 %collective-permute-start.18 = (f32[6,9,128]{2,1,0:T(8,128)S(1)}, f32[6,9,128]{2,1,0:T(8,128)S(1)}, u32[]{:S(2)}, u32[]{:S(2)}) collective-permute-start(f32[6,9,128]{2,1,0:T(8,128)S(1)} %get-tuple-element.401), channel_id=1, source_target_pairs={{0,1},{1,2},{2,3},{3,4},{4,5},{5,6},{6,7},{7,8},{8,9},{9,10},{10,1... | collective-permute-start | bytes 82952 | tf_op jit(solution)/shard_map/ppermute | solution.py:16
  448.8 14.6 %collective-permute-start.19 = (f32[6,9,128]{2,1,0:T(8,128)S(1)}, f32[6,9,128]{2,1,0:T(8,128)S(1)}, u32[]{:S(2)}, u32[]{:S(2)}) collective-permute-start(f32[6,9,128]{2,1,0:T(8,128)S(1)} %get-tuple-element.400), channel_id=1, source_target_pairs={{0,31},{1,0},{2,1},{3,2},{4,3},{5,4},{6,5},{7,6},{8,7},{9,8},{10,9... | collective-permute-start | bytes 82952 | tf_op jit(solution)/shard_map/ppermute | solution.py:16
  459.5 10.4 %collective-permute-start.22 = (f32[6,9,128]{2,1,0:T(8,128)S(1)}, f32[6,9,128]{2,1,0:T(8,128)S(1)}, u32[]{:S(2)}, u32[]{:S(2)}) collective-permute-start(f32[6,9,128]{2,1,0:T(8,128)S(1)} %get-tuple-element.398), channel_id=1, source_target_pairs={{0,1},{1,2},{2,3},{3,4},{4,5},{5,6},{6,7},{7,8},{8,9},{9,10},{10,1... | collective-permute-start | bytes 82952 | tf_op jit(solution)/shard_map/ppermute | solution.py:16
  461.5 10.7 %collective-permute-start.16 = (f32[6,9,128]{2,1,0:T(8,128)S(1)}, f32[6,9,128]{2,1,0:T(8,128)S(1)}, u32[]{:S(2)}, u32[]{:S(2)}) collective-permute-start(f32[6,9,128]{2,1,0:T(8,128)S(1)} %collective-permute-done.15), channel_id=1, source_target_pairs={{0,480},{32,0},{64,32},{96,64},{128,96},{160,128},{192,160},{224,1... | collective-permute-start | bytes 82952 | tf_op jit(solution)/shard_map/ppermute | solution.py:16
  463.4 15.2 %collective-permute-start.21 = (f32[6,9,128]{2,1,0:T(8,128)S(1)}, f32[6,9,128]{2,1,0:T(8,128)S(1)}, u32[]{:S(2)}, u32[]{:S(2)}) collective-permute-start(f32[6,9,128]{2,1,0:T(8,128)S(1)} %get-tuple-element.399), channel_id=1, source_target_pairs={{0,32},{32,64},{64,96},{96,128},{128,160},{160,192},{192,224},{224... | collective-permute-start | bytes 82952 | tf_op jit(solution)/shard_map/ppermute | solution.py:16
  469.9 8.7 %collective-permute-start.20 = (f32[6,9,128]{2,1,0:T(8,128)S(1)}, f32[6,9,128]{2,1,0:T(8,128)S(1)}, u32[]{:S(2)}, u32[]{:S(2)}) collective-permute-start(f32[6,9,128]{2,1,0:T(8,128)S(1)} %collective-permute-done.19), channel_id=1, source_target_pairs={{0,32},{32,64},{64,96},{96,128},{128,160},{160,192},{192,224},{224... | collective-permute-start | bytes 82952 | tf_op jit(solution)/shard_map/ppermute | solution.py:16
  472.2 9.0 %collective-permute-start.23 = (f32[6,9,128]{2,1,0:T(8,128)S(1)}, f32[6,9,128]{2,1,0:T(8,128)S(1)}, u32[]{:S(2)}, u32[]{:S(2)}) collective-permute-start(f32[6,9,128]{2,1,0:T(8,128)S(1)} %collective-permute-done.22), channel_id=1, source_target_pairs={{0,32},{32,64},{64,96},{96,128},{128,160},{160,192},{192,224},{224... | collective-permute-start | bytes 82952 | tf_op jit(solution)/shard_map/ppermute | solution.py:16
where the time goes:
time: 671 us; the launch traced here: 665 us
  other arithmetic  306 us (46%)
  local copies, waits for them, and re-layouts  124 us (18%)
  blocking collectives  109 us (16%)
  starting transfers between devices  94.9 us (14%)
  waiting for transfers between devices  22.3 us (3%)
  loops' own time  6.98 us (1%)
    pmax x1, blocking collectives, local(): global_top = lax.pmax(local_top, ('gx', 'yz'))  109 us
    ppermute x24, starting transfers between devices, shifted(): return lax.ppermute(value, axis, pairs)  94.9 us
    scatter-add x4, other arithmetic, nodal_velocity(): nodal.at[:, links[0]].add(half_force).at[:, links[1]].add(half_force)  93.2 us
    gather x80, local copies, waits for them, and re-layouts, group_step(): tile_terms = jax.vmap(tile_traction)(blocks[chosen[0]], sources[chosen[1]])  44.3 us
    reduce_sum x40, other arithmetic, tile_traction(): along = jnp.sum(across * burg_tgt, axis=0)  42.9 us
    gather x4, local copies, waits for them, and re-layouts, make_blocks(): first = jnp.take(points, links[0], axis=1)  32.7 us
    scatter-add x40, other arithmetic, group_step(): return running.at[chosen[0]].add(tile_terms)  31.1 us
    gather x4, local copies, waits for them, and re-layouts, make_blocks(): second = jnp.take(points, links[1], axis=1)  31 us
  transfers between devices with their start and end apart: 24, of which 7 were waited for; matrix products, arithmetic and copies ran while one was open for 0% of the time, Pallas kernels for 0%

commit v1 on v0

v1 whole, which is shorter than its diff:
```python
import functools

import jax
import jax.numpy as jnp
from jax import lax
from jax.experimental import pallas as pl
from jax.experimental.pallas import tpu as pltpu
from jax.sharding import PartitionSpec as P

F32 = jnp.float32
BF16 = jnp.bfloat16
A_SQUARED = 0.25
NU_FACTOR = 0.4
DX_LIMIT = 1.0
SPEED_EPS = 1e-05
DIRECTIONS = ((-1, -1), (-1, 0), (-1, 1), (0, -1), (0, 1), (1, -1), (1, 0), (1, 1))
BLK = 32
LANE = 128
GB = 6
SLOTS = BLK + 64
QROWS = 32
FROWS = 40
UNROLL = 4
MESH_ID = pl.DeviceIdType.MESH


def cross(u, v):
    return [u[1] * v[2] - u[2] * v[1], u[2] * v[0] - u[0] * v[2], u[0] * v[1] - u[1] * v[0]]


def dot3(u, v):
    return u[0] * v[0] + u[1] * v[1] + u[2] * v[2]


def rounded(x):
    return x.astype(BF16).astype(F32)


def split2(x):
    high = rounded(x)
    return high, rounded(x - high)


def split3(x):
    high = rounded(x)
    rest = x - high
    mid = rounded(rest)
    return high, mid, rounded(rest - mid)


def to_rows(src_ref, rows, stage_ref, lead=None):
    for k in range(BLK):
        lanes = pl.ds(k * LANE, LANE)
        piece = src_ref[:, lanes] if lead is None else src_ref[lead, :, lanes]
        stage_ref[8 * k : 8 * k + rows, :] = piece
    return [stage_ref[pl.ds(c, BLK, stride=8), :] for c in range(rows)]


def gather_ends(table_ref, ends):
    outs = []
    for end in ends:
        high = end >> 7
        low = end & 127
        picked = [jnp.zeros((BLK, LANE), F32) for _ in range(3)]
        for row in range(BLK):
            here = high == row
            for c in range(3):
                wide = jnp.broadcast_to(table_ref[c, row : row + 1, :], (BLK, LANE))
                found = jnp.take_along_axis(wide, low, axis=1, mode="promise_in_bounds")
                picked[c] = jnp.where(here, found, picked[c])
        outs.append(picked)
    return outs


def pack_blocks(send_list, block_ref, rows, send_ref):
    for k in range(8):
        for g in range(GB):
            chosen = send_list[0, k, g]
            send_ref[k, rows * g : rows * (g + 1), :] = block_ref[chosen, 0:rows, :]


def prepare_kernel(send_list, nodes_ref, links_ref, burgers_ref, own_ref, ends_ref, send_ref, stage_ref, table_ref, block_ref):
    coords = to_rows(nodes_ref, 3, stage_ref)
    for c in range(3):
        table_ref[c] = coords[c]
    for k in range(BLK):
        lanes = pl.ds(k * LANE, LANE)
        ends_ref[0, k : k + 1, :] = links_ref[0:1, lanes]
        ends_ref[1, k : k + 1, :] = links_ref[1:2, lanes]
    first, second = gather_ends(table_ref, [ends_ref[0], ends_ref[1]])
    burgers = to_rows(burgers_ref, 3, stage_ref)
    rows = [0.5 * (first[c] + second[c]) for c in range(3)] + [second[c] - first[c] for c in range(3)] + burgers
    for c in range(9):
        own_ref[c] = rows[c]
        for k in range(BLK):
            block_ref[k, c : c + 1, :] = rows[c][k : k + 1]
    pack_blocks(send_list, block_ref, 9, send_ref)


def neighbours():
    gx = lax.axis_index("gx")
    yz = lax.axis_index("yz")
    n_gx = lax.axis_size("gx")
    n_yz = lax.axis_size("yz")
    return [(lax.rem(gx + dx + n_gx, n_gx), lax.rem(yz + dy + n_yz, n_yz)) for dx, dy in DIRECTIONS]


def greet(targets):
    barrier = pltpu.get_barrier_semaphore()
    for target in targets:
        pl.semaphore_signal(barrier, inc=1, device_id=target, device_id_type=MESH_ID)
    pl.semaphore_wait(barrier, len(targets))


def ghost_copies(send_ref, recv_ref, send_sem, recv_sem, targets):
    return [
        pltpu.make_async_remote_copy(
            src_ref=send_ref.at[k],
            dst_ref=recv_ref.at[k],
            send_sem=send_sem.at[k],
            recv_sem=recv_sem.at[k],
            device_id=targets[k],
            device_id_type=MESH_ID,
        )
        for k in range(8)
    ]


def exchange_kernel(send_ref, recv_ref, send_sem, recv_sem):
    targets = neighbours()
    greet(targets)
    copies = ghost_copies(send_ref, recv_ref, send_sem, recv_sem, targets)
    for copy in copies:
        copy.start()
    for copy in copies:
        copy.wait()


def exchange_max_kernel(n_gx, n_yz, send_ref, top_ref, recv_ref, out_ref, box_gx, box_yz, mid_ref, send_sem, recv_sem, sgx, rgx, syz, ryz):
    targets = neighbours()
    gx = lax.axis_index("gx")
    yz = lax.axis_index("yz")
    line_gx = [(lax.rem(gx + o, n_gx), yz) for o in range(1, n_gx)]
    line_yz = [(gx, lax.rem(yz + o, n_yz)) for o in range(1, n_yz)]
    corners = [targets[k] for k in (0, 2, 5, 7)]
    greet(line_gx + line_yz + corners)

    def spread(source, box, send, recv, line):
        return [
            pltpu.make_async_remote_copy(
                src_ref=source,
                dst_ref=box.at[o + 1],
                send_sem=send.at[o + 1],
                recv_sem=recv.at[o + 1],
                device_id=line[o],
                device_id_type=MESH_ID,
            )
            for o in range(len(line))
        ]

    along_gx = spread(top_ref, box_gx, sgx, rgx, line_gx)
    for copy in along_gx:
        copy.start()
    copies = ghost_copies(send_ref, recv_ref, send_sem, recv_sem, targets)
    for copy in copies:
        copy.start()
    best = top_ref[...]
    for copy in along_gx:
        copy.wait_recv()
    for o in range(1, n_gx):
        best = jnp.maximum(best, box_gx[o])
    mid_ref[...] = best
    along_yz = spread(mid_ref, box_yz, syz, ryz, line_yz)
    for copy in along_yz:
        copy.start()
    for copy in along_yz:
        copy.wait_recv()
    for o in range(1, n_yz):
        best = jnp.maximum(best, box_yz[o])
    out_ref[...] = best
    for copy in along_gx:
        copy.wait_send()
    for copy in along_yz:
        copy.wait_send()
    for copy in copies:
        copy.wait()


def source_features(mid, line, burg, slot, qs_ref, f_ref):
    def put_q(row, value):
        qs_ref[pl.ds(slot * QROWS + row, BLK, stride=QROWS), :] = value

    def put_f(row, value):
        f_ref[pl.ds(slot * FROWS + row, BLK, stride=FROWS), :] = value

    row = 0
    for c in range(3):
        high, middle, low = split3(mid[c])
        for part in (high, high, middle, middle, high, low):
            put_q(row, part)
            row += 1
    for part in split3(dot3(mid, mid) + A_SQUARED):
        put_q(row, part)
        row += 1
    one = jnp.ones((BLK, LANE), F32)
    zero = jnp.zeros((BLK, LANE), F32)
    for _ in range(3):
        put_q(row, one)
        row += 1
    while row < QROWS:
        put_q(row, zero)
        row += 1
    moment = cross(burg, mid)
    for a in range(3):
        for d in range(3):
            high, low = split2(line[a] * burg[d])
            put_f(3 * a + d, high)
            put_f(18 + 3 * a + d, low)
            high, low = split2(line[a] * moment[d])
            put_f(9 + 3 * a + d, high)
            put_f(27 + 3 * a + d, low)


def target_features(mid, qt_ref):
    def put(row, value):
        qt_ref[pl.ds(row, BLK, stride=QROWS), :] = value

    row = 0
    for c in range(3):
        high, middle, low = split3(-2.0 * mid[c])
        for part in (high, middle, high, middle, low, high):
            put(row, part)
            row += 1
    one = jnp.ones((BLK, LANE), F32)
    zero = jnp.zeros((BLK, LANE), F32)
    for _ in range(3):
        put(row, one)
        row += 1
    for part in split3(dot3(mid, mid)):
        put(row, part)
        row += 1
    while row < QROWS:
        put(row, zero)
        row += 1


def velocity(own, ghost, pairs, count, ends_ref, mob_ref, scr):
    qs_f, qt_f, f_f, qs_b, qt_b, f_b, acc, force_ref = scr
    centre = [jnp.mean(own[c]) for c in range(3)]
    mid = [own[c] - centre[c] for c in range(3)]
    line = own[3:6]
    burg = own[6:9]
    source_features(mid, line, burg, 0, qs_f, f_f)
    target_features(mid, qt_f)
    for half in range(2):
        rows = [ghost(c, half) for c in range(9)]
        source_features([rows[c] - centre[c] for c in range(3)], rows[3:6], rows[6:9], BLK * (half + 1), qs_f, f_f)

    def convert(step, carry):
        for j in range(4):
            slot = 4 * step + j
            q = qs_f[pl.ds(pl.multiple_of(slot * QROWS, 8), QROWS), :]
            qs_b[slot] = jnp.transpose(q).astype(BF16)
            f = f_f[pl.ds(pl.multiple_of(slot * FROWS, 8), FROWS), :].astype(BF16)
            f_b[slot] = jnp.concatenate([f, f], axis=1)
        return carry

    lax.fori_loop(0, SLOTS // 4, convert, 0)

    def convert_target(step, carry):
        for j in range(4):
            slot = 4 * step + j
            qt_b[slot] = qt_f[pl.ds(pl.multiple_of(slot * QROWS, 8), QROWS), :].astype(BF16)
        return carry

    lax.fori_loop(0, BLK // 4, convert_target, 0)
    acc[...] = jnp.zeros(acc.shape, F32)

    def pair_step(step, carry):
        found = []
        for j in range(UNROLL):
            place = UNROLL * step + j
            live = place < count
            target = jnp.where(live, pairs[0, place], BLK)
            source = jnp.where(live, pairs[1, place], 0)
            ghost_place = source - BLK
            group = (ghost_place * 43) >> 8
            slot = jnp.where(source < BLK, source, BLK + 8 * group + (ghost_place - GB * group))
            dist = jnp.dot(qs_b[slot], qt_b[target], preferred_element_type=F32)
            root = lax.rsqrt(dist)
            weight = root * root * root
            high = weight.astype(BF16)
            low = (weight - high.astype(F32)).astype(BF16)
            both = jnp.concatenate([high, low], axis=0)
            found.append((target, jnp.dot(f_b[slot], both, preferred_element_type=F32)))
        for target, part in found:
            acc[target] += part
        return carry

    lax.fori_loop(0, (count + UNROLL - 1) // UNROLL, pair_step, 0)

    def total(row):
        return acc[0:BLK, row, :] + acc[0:BLK, row + 18, :]

    s_mat = [[total(3 * a + d) for d in range(3)] for a in range(3)]
    t_mat = [[total(9 + 3 * a + d) for d in range(3)] for a in range(3)]
    arm = cross(mid, burg)
    lined_s = [burg[0] * s_mat[0][d] + burg[1] * s_mat[1][d] + burg[2] * s_mat[2][d] for d in range(3)]
    lined_t = [burg[0] * t_mat[0][d] + burg[1] * t_mat[1][d] + burg[2] * t_mat[2][d] for d in range(3)]
    swept = cross(lined_s, mid)
    skew = [s_mat[2][1] - s_mat[1][2], s_mat[0][2] - s_mat[2][0], s_mat[1][0] - s_mat[0][1]]
    twist = NU_FACTOR * (dot3(mid, skew) + (t_mat[0][0] + t_mat[1][1] + t_mat[2][2]))
    traction = [
        0.5 * ((dot3(s_mat[k], arm) - dot3(t_mat[k], burg)) + (swept[k] - lined_t[k])) + twist * burg[k]
        for k in range(3)
    ]
    force = cross(traction, line)
    for c in range(3):
        high, low = split2(0.5 * force[c])
        force_ref[2 * c] = high
        force_ref[2 * c + 1] = low

    row_id = lax.broadcasted_iota(jnp.int32, (BLK, LANE), 0)
    lane_id = lax.broadcasted_iota(jnp.int32, (LANE, LANE), 0)

    def scatter_step(k, nodal):
        lhs = []
        rhs = []
        for e in range(2):
            end = ends_ref[e, pl.ds(k, 1), :]
            here = row_id == (end >> 7)
            lhs.append(
                jnp.concatenate(
                    [jnp.where(here, force_ref[i, pl.ds(k, 1), :], 0.0).astype(BF16) for i in range(6)], axis=0
                )
            )
            rhs.append(jnp.where(lane_id == (end & 127), 1.0, 0.0).astype(BF16))
        return nodal + lax.dot_general(
            jnp.concatenate(lhs, axis=1),
            jnp.concatenate(rhs, axis=1),
            (((1,), (1,)), ((), ())),
            preferred_element_type=F32,
        )

    nodal = lax.fori_loop(0, BLK, scatter_step, jnp.zeros((6 * BLK, LANE), F32))
    pulled = [nodal[2 * BLK * c : 2 * BLK * c + BLK] + nodal[2 * BLK * c + BLK : 2 * BLK * (c + 1)] for c in range(3)]
    return [dot3([mob_ref[3 * r + c] for c in range(3)], pulled) for r in range(3)]


def first_kernel(
    send_list, pairs, count, own_ref, recv_ref, ends_ref, mobility_ref,
    v_ref, top_ref, own_v_ref, send_ref, ghost_ref, mob_ref, stage_ref, block_ref, *scr
):
    for r in range(3):
        rows = to_rows(mobility_ref, 3, stage_ref, r)
        for c in range(3):
            mob_ref[3 * r + c] = rows[c]
    for c in range(9):
        for k in range(8):
            ghost_ref[c, 8 * k : 8 * k + GB, :] = recv_ref[k, pl.ds(c, GB, stride=9), :]
            ghost_ref[c, 8 * k + GB : 8 * k + 8, :] = jnp.zeros((8 - GB, LANE), F32)
    own = [own_ref[c] for c in range(9)]
    speed = velocity(own, lambda c, half: ghost_ref[c, BLK * half : BLK * (half + 1), :], pairs, count[0], ends_ref, mob_ref, scr)
    for c in range(3):
        v_ref[c] = speed[c]
    top_ref[...] = jnp.max(dot3(speed, speed), axis=0, keepdims=True)
    first, second = gather_ends(v_ref, [ends_ref[0], ends_ref[1]])
    rows = [0.5 * (first[c] + second[c]) for c in range(3)] + [second[c] - first[c] for c in range(3)]
    for c in range(6):
        own_v_ref[c] = rows[c]
        for k in range(BLK):
            block_ref[k, c : c + 1, :] = rows[c][k : k + 1]
    pack_blocks(send_list, block_ref, 6, send_ref)


def second_kernel(
    pairs, count, own_ref, ghost_ref, own_v_ref, recv_ref, top_ref, v_ref, ends_ref, mob_ref,
    out_ref, moved_ref, stage_ref, *scr
):
    step = DX_LIMIT / (jnp.sqrt(jnp.max(top_ref[...])) + SPEED_EPS)
    for c in range(9):
        if c < 6:
            for k in range(8):
                rows = slice(8 * k, 8 * k + GB)
                moved_ref[c, rows, :] = ghost_ref[c, rows, :] + step * recv_ref[k, pl.ds(c, GB, stride=6), :]
                moved_ref[c, 8 * k + GB : 8 * k + 8, :] = jnp.zeros((8 - GB, LANE), F32)
        else:
            moved_ref[c] = ghost_ref[c]
    own = [own_ref[c] + step * own_v_ref[c] if c < 6 else own_ref[c] for c in range(9)]
    speed = velocity(own, lambda c, half: moved_ref[c, BLK * half : BLK * (half + 1), :], pairs, count[0], ends_ref, mob_ref, scr)
    for c in range(3):
        stage_ref[pl.ds(c, BLK, stride=8), :] = 0.5 * step * (v_ref[c] + speed[c])
    for k in range(BLK):
        out_ref[:, pl.ds(k * LANE, LANE)] = stage_ref[8 * k : 8 * k + 3, :]


VMEM = pl.BlockSpec(memory_space=pltpu.VMEM)
SMEM = pl.BlockSpec(memory_space=pltpu.SMEM)
DMA = pltpu.SemaphoreType.DMA


def shape(*dims, dtype=F32):
    return jax.ShapeDtypeStruct(dims, dtype)


def velocity_scratch():
    return [
        pltpu.VMEM((SLOTS * QROWS, LANE), F32),
        pltpu.VMEM((BLK * QROWS, LANE), F32),
        pltpu.VMEM((SLOTS * FROWS, LANE), F32),
        pltpu.VMEM((SLOTS, LANE, QROWS), BF16),
        pltpu.VMEM((BLK + 1, QROWS, LANE), BF16),
        pltpu.VMEM((SLOTS, FROWS, 2 * LANE), BF16),
        pltpu.VMEM((BLK + 1, FROWS, LANE), F32),
        pltpu.VMEM((6, BLK, LANE), F32),
    ]


STAGE = pltpu.VMEM((BLK * 8, LANE), F32)
BLOCKS = pltpu.VMEM((BLK, 16, LANE), F32)
LOCAL = pltpu.CompilerParams(vmem_limit_bytes=40 * 1024 * 1024)


def prepare(send_list, nodes, links, burgers):
    return pl.pallas_call(
        prepare_kernel,
        out_shape=(shape(9, BLK, LANE), shape(2, BLK, LANE, dtype=jnp.int32), shape(8, 9 * GB, LANE)),
        in_specs=[SMEM, VMEM, VMEM, VMEM],
        out_specs=(VMEM, VMEM, VMEM),
        scratch_shapes=[STAGE, pltpu.VMEM((3, BLK, LANE), F32), BLOCKS],
        compiler_params=LOCAL,
        name="prepare",
    )(send_list, nodes, links, burgers)


def exchange(send):
    return pl.pallas_call(
        exchange_kernel,
        out_shape=shape(*send.shape),
        in_specs=[VMEM],
        out_specs=VMEM,
        scratch_shapes=[DMA((8,)), DMA((8,))],
        compiler_params=pltpu.CompilerParams(collective_id=0, has_side_effects=True, vmem_limit_bytes=4 * 1024 * 1024),
        name="exchange",
    )(send)


def exchange_max(send, top):
    n_gx = lax.axis_size("gx")
    n_yz = lax.axis_size("yz")
    return pl.pallas_call(
        functools.partial(exchange_max_kernel, n_gx, n_yz),
        out_shape=(shape(*send.shape), shape(1, LANE)),
        in_specs=[VMEM, VMEM],
        out_specs=(VMEM, VMEM),
        scratch_shapes=[
            pltpu.VMEM((n_gx, 1, LANE), F32),
            pltpu.VMEM((n_yz, 1, LANE), F32),
            pltpu.VMEM((1, LANE), F32),
            DMA((8,)), DMA((8,)), DMA((n_gx,)), DMA((n_gx,)), DMA((n_yz,)), DMA((n_yz,)),
        ],
        compiler_params=pltpu.CompilerParams(collective_id=1, has_side_effects=True, vmem_limit_bytes=4 * 1024 * 1024),
        name="exchange_max",
    )(send, top)


def first(send_list, pairs, count, own, recv, ends, mobility):
    return pl.pallas_call(
        first_kernel,
        out_shape=(
            shape(3, BLK, LANE), shape(1, LANE), shape(6, BLK, LANE), shape(8, 6 * GB, LANE),
            shape(9, 64, LANE), shape(9, BLK, LANE),
        ),
        in_specs=[SMEM, SMEM, SMEM, VMEM, VMEM, VMEM, VMEM],
        out_specs=(VMEM,) * 6,
        scratch_shapes=[STAGE, BLOCKS] + velocity_scratch(),
        compiler_params=LOCAL,
        name="first",
    )(send_list, pairs, count, own, recv, ends, mobility)


def second(pairs, count, own, ghost, own_v, recv, top, v, ends, mob):
    return pl.pallas_call(
        second_kernel,
        out_shape=shape(3, BLK * LANE),
        in_specs=[SMEM, SMEM] + [VMEM] * 8,
        out_specs=VMEM,
        scratch_shapes=[pltpu.VMEM((9, 64, LANE), F32), STAGE] + velocity_scratch(),
        compiler_params=LOCAL,
        name="second",
    )(pairs, count, own, ghost, own_v, recv, top, v, ends, mob)


def local(nodes, links, burgers, mobility, send_list, pair_list, pair_count):
    own, ends, send = prepare(send_list, nodes, links, burgers)
    recv = exchange(send)
    v, top, own_v, send_v, ghost, mob = first(send_list, pair_list, pair_count, own, recv, ends, mobility)
    recv_v, top_all = exchange_max(send_v, top)
    return second(pair_list, pair_count, own, ghost, own_v, recv_v, top_all, v, ends, mob)


def solution(mesh):
    return jax.shard_map(
        local,
        mesh=mesh,
        in_specs=(
            P(None, ("gx", "yz")),
            P(None, ("gx", "yz")),
            P(None, ("gx", "yz")),
            P(None, None, ("gx", "yz")),
            P(("gx", "yz"), None, None),
            P(None, ("gx", "yz")),
            P(("gx", "yz")),
        ),
        out_specs=P(None, ("gx", "yz")),
        check_vma=False,
    )
```

time: 671 us -> 102 us (0.15)
  the two profiles are of different devices: /device:TPU:1 before, /device:TPU:32 now
where the time goes in v1:
time: 102 us
  Pallas kernels  97.9 us (96%)
  local copies, waits for them, and re-layouts  3.21 us (3%)
    pallas_call x1, Pallas kernels, first(): pl.pallas_call(first_kernel, out_shape=(shape(3, BLK, LANE), shape(1, LAN...  27.3 us
    pallas_call x1, Pallas kernels, second(): pl.pallas_call(second_kernel, out_shape=shape(3, BLK * LANE), in_specs=[S...  25.7 us
    pallas_call x1, Pallas kernels, exchange_max(): pl.pallas_call(functools.partial(exchange_max_kernel, n_gx, n_yz), out_sh...  21.6 us
    pallas_call x1, Pallas kernels, exchange(): pl.pallas_call(exchange_kernel, out_shape=shape(*send.shape), in_specs=[V...  20.5 us
    unnamed x11, local copies, waits for them, and re-layouts  3.21 us
    pallas_call x1, Pallas kernels, prepare(): pl.pallas_call(prepare_kernel, out_shape=(shape(9, BLK, LANE), shape(2, B...  2.91 us

profile of v1, /device:TPU:32, one launch (start us, length us, event | category | flops | bytes accessed | tf_op | source)
XLA Modules:
  0.0 101.8 jit_solution(619675548369779963)
XLA Ops:
  0.7 0.8 copy.8.send_list
  1.4 0.0 copy-start.1
  1.4 0.8 copy-done.1
  2.3 0.0 copy-start.2
  2.3 0.8 copy-done.2
  3.1 0.0 copy-start.3
  3.1 0.8 copy-done.3
  3.9 2.9 %prepare.1 = (f32[9,32,128]{2,1,0:T(8,128)S(1)}, s32[2,32,128]{2,1,0:T(8,128)S(1)}, f32[8,54,128]{2,1,0:T(8,128)S(1)}) custom-call(s32[1,8,6]{2,1,0:T(8,128)S(1)} %copy.8.send_list, f32[3,4096]{1,0:T(4,128)S(1)} %copy-done.1, s32[2,4096]{1,0:T(2,128)S(1)} %copy-done.3, f32[3,4096]{1,0:T(4,128)S(1)} %copy-done.2), custom_call_target="tpu_custom_call" | custom-call | tf_op jit(solution)/shard_map/prepare/pallas_call | solution.py:425
  6.8 0.0 copy-start
  6.8 0.0 copy-start.4
  6.8 20.5 %exchange.1.recv_ref = f32[8,54,128]{2,1,0:T(8,128)S(1)} custom-call(f32[8,54,128]{2,1,0:T(8,128)S(1)} %get-tuple-element.17.send_ref), custom_call_target="tpu_custom_call" | custom-call | tf_op jit(solution)/shard_map/exchange/pallas_call | solution.py:437
  27.3 0.0 copy-done
  27.3 0.0 copy-done.4
  27.3 27.3 %first.1 = (f32[3,32,128]{2,1,0:T(8,128)S(1)}, f32[1,128]{1,0:T(1,128)S(1)}, f32[6,32,128]{2,1,0:T(8,128)S(1)}, f32[8,36,128]{2,1,0:T(8,128)S(1)}, f32[9,64,128]{2,1,0:T(8,128)S(1)}, /*index=5*/f32[9,32,128]{2,1,0:T(8,128)S(1)}) custom-call(s32[1,8,6]{2,1,0:T(8,128)S(1)} %copy.8.send_list, s32[2,160]{1,0:T(2,128)S(1)} %copy-done.4, s32[1]{0:T(128)S(6)} %copy.10.count, ...), custom_call_target="tpu_custom_call" | custom-call | tf_op jit(solution)/shard_map/first/pallas_call | solution.py:468
  54.6 21.6 %exchange_max.1 = (f32[8,36,128]{2,1,0:T(8,128)S(1)}, f32[1,128]{1,0:T(1,128)S(1)}) custom-call(f32[8,36,128]{2,1,0:T(8,128)S(1)} %get-tuple-element.21.send_ref, f32[1,128]{1,0:T(1,128)S(1)} %get-tuple-element.22.top_ref), custom_call_target="tpu_custom_call" | custom-call | tf_op jit(solution)/shard_map/exchange_max/pallas_call | solution.py:451
  76.2 25.7 %second.1 = f32[3,4096]{1,0:T(4,128)} custom-call(s32[2,160]{1,0:T(2,128)S(1)} %copy-done.4, s32[1]{0:T(128)S(6)} %copy.10.count, f32[9,32,128]{2,1,0:T(8,128)S(1)} %get-tuple-element.16.own_ref, f32[9,64,128]{2,1,0:T(8,128)S(1)} %get-tuple-element.19.ghost_ref, f32[6,32,128]{2,1,0:T(8,128)S(1)} %get-tuple-element.20.own_v_ref, ...), custom_call_target="tpu_custom_call" | custom-call | tf_op jit(solution)/shard_map/second/pallas_call | solution.py:483
Async XLA Ops:
  1.4 0.8 copy-start.1
  2.3 0.8 copy-start.2
  3.1 0.8 copy-start.3
  6.8 20.5 %copy-start = (f32[3,3,4096]{2,1,0:T(4,128)S(1)}, f32[3,3,4096]{2,1,0:T(4,128)}, u32[]{:S(2)}) copy-start(f32[3,3,4096]{2,1,0:T(4,128)} %mobility_ref.1) | copy-start | bytes 442372
  6.8 20.5 %copy-start.4 = (s32[2,160]{1,0:T(2,128)S(1)}, s32[2,160]{1,0:T(2,128)}, u32[]{:S(2)}) copy-start(s32[2,160]{1,0:T(2,128)} %pairs.3) | copy-start | bytes 3844

commit v2 on v1

v2 whole, which is shorter than its diff:
```python
import functools
import itertools
import math

import jax
import jax.numpy as jnp
from jax import lax
from jax.experimental import pallas as pl
from jax.experimental.pallas import tpu as pltpu
from jax.sharding import PartitionSpec as P

F32 = jnp.float32
BF16 = jnp.bfloat16
A_SQUARED = 0.25
NU_FACTOR = 0.4
DX_LIMIT = 1.0
SPEED_EPS = 1e-05
DIRECTIONS = ((-1, -1), (-1, 0), (-1, 1), (0, -1), (0, 1), (1, -1), (1, 0), (1, 1))
BLK = 32
LANE = 128
GB = 6
SLOTS = BLK + 64
QROWS = 32
FROWS = 48
UNROLL = 16
SCAT = 8
PAIRS = 160
MESH_ID = pl.DeviceIdType.MESH
STAGES = ((("yz", 1, 2),), (("gx", 1, 4), ("yz", 2, 4)), (("gx", 4, 4), ("yz", 8, 4)))


def cross(u, v):
    return [u[1] * v[2] - u[2] * v[1], u[2] * v[0] - u[0] * v[2], u[0] * v[1] - u[1] * v[0]]


def dot3(u, v):
    return u[0] * v[0] + u[1] * v[1] + u[2] * v[2]


def rounded(x):
    return x.astype(BF16).astype(F32)


def split2(x):
    high = rounded(x)
    return high, rounded(x - high)


def split3(x):
    high = rounded(x)
    rest = x - high
    mid = rounded(rest)
    return high, mid, rounded(rest - mid)


def to_rows(src_ref, rows, stage_ref, lead=None):
    for k in range(BLK):
        lanes = pl.ds(k * LANE, LANE)
        piece = src_ref[:, lanes] if lead is None else src_ref[lead, :, lanes]
        stage_ref[8 * k : 8 * k + rows, :] = piece
    return [stage_ref[pl.ds(c, BLK, stride=8), :] for c in range(rows)]


def gather_ends(table_ref, ends):
    outs = []
    for end in ends:
        high = end >> 7
        low = end & 127
        picked = [jnp.zeros((BLK, LANE), F32) for _ in range(3)]
        for row in range(BLK):
            here = high == row
            for c in range(3):
                wide = jnp.broadcast_to(table_ref[c, row : row + 1, :], (BLK, LANE))
                found = jnp.take_along_axis(wide, low, axis=1, mode="promise_in_bounds")
                picked[c] = jnp.where(here, found, picked[c])
        outs.append(picked)
    return outs


def pack_blocks(send_list, block_ref, rows, send_ref):
    for k in range(8):
        for g in range(GB):
            chosen = send_list[g, 0, k]
            send_ref[k, rows * g : rows * (g + 1), :] = block_ref[chosen, 0:rows, :]


def digits(stage):
    place = {"gx": lax.axis_index("gx"), "yz": lax.axis_index("yz")}
    found = []
    for offsets in itertools.product(*[range(size) for _, _, size in stage]):
        if any(offsets):
            peer = dict(place)
            for (axis, stride, size), offset in zip(stage, offsets):
                digit = lax.rem(lax.div(place[axis], stride), size)
                peer[axis] = peer[axis] + (lax.rem(digit + offset, size) - digit) * stride
            found.append((peer["gx"], peer["yz"]))
    return found


def neighbours():
    gx = lax.axis_index("gx")
    yz = lax.axis_index("yz")
    n_gx = lax.axis_size("gx")
    n_yz = lax.axis_size("yz")
    return [(lax.rem(gx + dx + n_gx, n_gx), lax.rem(yz + dy + n_yz, n_yz)) for dx, dy in DIRECTIONS]


def remote(source, target, send_sem, recv_sem, device):
    return pltpu.make_async_remote_copy(
        src_ref=source, dst_ref=target, send_sem=send_sem, recv_sem=recv_sem, device_id=device, device_id_type=MESH_ID
    )


def ghost_copies(send_ref, recv_ref, send_sem, recv_sem, targets):
    return [remote(send_ref.at[k], recv_ref.at[k], send_sem.at[k], recv_sem.at[k], targets[k]) for k in range(8)]


def source_features(mid, line, burg, slot, qs_ref, f_ref):
    def put_q(row, value):
        qs_ref[pl.ds(slot * QROWS + row, BLK, stride=QROWS), :] = value

    def put_f(row, value):
        f_ref[pl.ds(slot * FROWS + row, BLK, stride=FROWS), :] = value

    row = 0
    for c in range(3):
        high, middle, low = split3(mid[c])
        for part in (high, high, middle, middle, high, low):
            put_q(row, part)
            row += 1
    for part in split3(dot3(mid, mid) + A_SQUARED):
        put_q(row, part)
        row += 1
    one = jnp.ones((BLK, LANE), F32)
    zero = jnp.zeros((BLK, LANE), F32)
    for _ in range(3):
        put_q(row, one)
        row += 1
    while row < QROWS:
        put_q(row, zero)
        row += 1
    moment = cross(burg, mid)
    for a in range(3):
        for d in range(3):
            high, low = split2(line[a] * burg[d])
            put_f(3 * a + d, high)
            put_f(24 + 3 * a + d, low)
            high, low = split2(line[a] * moment[d])
            put_f(9 + 3 * a + d, high)
            put_f(33 + 3 * a + d, low)


def target_features(mid, qt_ref):
    def put(row, value):
        qt_ref[pl.ds(row, BLK, stride=QROWS), :] = value

    row = 0
    for c in range(3):
        high, middle, low = split3(-2.0 * mid[c])
        for part in (high, middle, high, middle, low, high):
            put(row, part)
            row += 1
    one = jnp.ones((BLK, LANE), F32)
    zero = jnp.zeros((BLK, LANE), F32)
    for _ in range(3):
        put(row, one)
        row += 1
    for part in split3(dot3(mid, mid)):
        put(row, part)
        row += 1
    while row < QROWS:
        put(row, zero)
        row += 1


def velocity(own, fill_ghost, ghost, pairs, pair_row, count, ends_ref, mob_ref, scr):
    qs_f, qt_f, f_f, qs_b, qt_b, f_b, acc, force_ref = scr
    centre = [jnp.mean(own[c]) for c in range(3)]
    mid = [own[c] - centre[c] for c in range(3)]
    line = own[3:6]
    burg = own[6:9]
    source_features(mid, line, burg, 0, qs_f, f_f)
    target_features(mid, qt_f)
    fill_ghost()
    for half in range(2):
        rows = [ghost(c, half) for c in range(9)]
        source_features([rows[c] - centre[c] for c in range(3)], rows[3:6], rows[6:9], BLK * (half + 1), qs_f, f_f)

    def convert(step, carry):
        for j in range(4):
            slot = 4 * step + j
            q = qs_f[pl.ds(pl.multiple_of(slot * QROWS, 8), QROWS), :]
            qs_b[slot] = jnp.transpose(q).astype(BF16)
            f = f_f[pl.ds(pl.multiple_of(slot * FROWS, 8), FROWS), :].astype(BF16)
            f_b[slot] = jnp.concatenate([f, f], axis=1)
        return carry

    lax.fori_loop(0, SLOTS // 4, convert, 0)

    def convert_target(step, carry):
        for j in range(4):
            slot = 4 * step + j
            qt_b[slot] = qt_f[pl.ds(pl.multiple_of(slot * QROWS, 8), QROWS), :].astype(BF16)
        return carry

    lax.fori_loop(0, BLK // 4, convert_target, 0)
    def pair_step(step, carry):
        for j in range(UNROLL):
            place = UNROLL * step + j
            target = jnp.minimum(pairs[0, place], BLK - 1)
            source = pairs[1, place]
            ghost_place = source - BLK
            group = (ghost_place * 43) >> 8
            slot = jnp.where(source < BLK, source, BLK + 8 * group + (ghost_place - GB * group))
            dist = jnp.dot(qs_b[slot], qt_b[target], preferred_element_type=F32)
            root = lax.rsqrt(dist)
            weight = root * root * root
            high = weight.astype(BF16)
            low = (weight - high.astype(F32)).astype(BF16)
            both = jnp.concatenate([high, low], axis=0)
            found = jnp.dot(f_b[slot], both, preferred_element_type=F32)
            acc[:, place, :] = found[0:24] + found[24:48]
        return carry

    lax.fori_loop(0, PAIRS // UNROLL, pair_step, 0)
    pair_id = lax.broadcasted_iota(jnp.int32, (BLK, PAIRS), 1)
    block_id = lax.broadcasted_iota(jnp.int32, (BLK, PAIRS), 0)
    chosen = jnp.where((block_id == pair_row[0:1, :]) & (pair_id < count), 1.0, 0.0).astype(BF16)
    chosen = jnp.concatenate([chosen, chosen], axis=1)

    def total(row):
        high = acc[row].astype(BF16)
        low = (acc[row] - high.astype(F32)).astype(BF16)
        return jnp.dot(chosen, jnp.concatenate([high, low], axis=0), preferred_element_type=F32)

    s_mat = [[total(3 * a + d) for d in range(3)] for a in range(3)]
    t_mat = [[total(9 + 3 * a + d) for d in range(3)] for a in range(3)]
    arm = cross(mid, burg)
    lined_s = [burg[0] * s_mat[0][d] + burg[1] * s_mat[1][d] + burg[2] * s_mat[2][d] for d in range(3)]
    lined_t = [burg[0] * t_mat[0][d] + burg[1] * t_mat[1][d] + burg[2] * t_mat[2][d] for d in range(3)]
    swept = cross(lined_s, mid)
    skew = [s_mat[2][1] - s_mat[1][2], s_mat[0][2] - s_mat[2][0], s_mat[1][0] - s_mat[0][1]]
    twist = NU_FACTOR * (dot3(mid, skew) + (t_mat[0][0] + t_mat[1][1] + t_mat[2][2]))
    traction = [
        0.5 * ((dot3(s_mat[k], arm) - dot3(t_mat[k], burg)) + (swept[k] - lined_t[k])) + twist * burg[k]
        for k in range(3)
    ]
    force = cross(traction, line)
    for c in range(3):
        high, low = split2(0.5 * force[c])
        force_ref[2 * c] = high
        force_ref[2 * c + 1] = low

    row_id = lax.broadcasted_iota(jnp.int32, (BLK, LANE), 0)
    lane_id = lax.broadcasted_iota(jnp.int32, (LANE, LANE), 0)

    def scatter_step(step, nodal):
        lhs = []
        rhs = []
        for j in range(SCAT):
            k = SCAT * step + j
            for e in range(2):
                end = ends_ref[e, pl.ds(k, 1), :]
                here = row_id == (end >> 7)
                lhs.append(
                    jnp.concatenate(
                        [jnp.where(here, force_ref[i, pl.ds(k, 1), :], 0.0).astype(BF16) for i in range(6)], axis=0
                    )
                )
                rhs.append(jnp.where(lane_id == (end & 127), 1.0, 0.0).astype(BF16))
        return nodal + lax.dot_general(
            jnp.concatenate(lhs, axis=1),
            jnp.concatenate(rhs, axis=1),
            (((1,), (1,)), ((), ())),
            preferred_element_type=F32,
        )

    nodal = lax.fori_loop(0, BLK // SCAT, scatter_step, jnp.zeros((6 * BLK, LANE), F32))
    pulled = [nodal[2 * BLK * c : 2 * BLK * c + BLK] + nodal[2 * BLK * c + BLK : 2 * BLK * (c + 1)] for c in range(3)]
    return [dot3([mob_ref[3 * r + c] for c in range(3)], pulled) for r in range(3)]


def step_kernel(
    stages, send_list, pairs, count_ref, pair_row, nodes_hbm, links_hbm, burgers_hbm, mobility_hbm, out_ref,
    nodes_ref, links_ref, burgers_ref, mobility_ref, in_sem,
    own_ref, own_v_ref, v_ref, ends_ref, mob_ref, ghost_ref, stage_ref, block_ref,
    send_ref, recv_ref, send_v_ref, recv_v_ref, box_ref, mid_ref, gs1, gr1, gs2, gr2, ms, mr, *scr
):
    loads = [
        pltpu.make_async_copy(src, dst, in_sem.at[i])
        for i, (src, dst) in enumerate(
            ((nodes_hbm, nodes_ref), (links_hbm, links_ref), (burgers_hbm, burgers_ref), (mobility_hbm, mobility_ref))
        )
    ]
    for load in loads:
        load.start()
    targets = neighbours()
    lines = [digits(stage) for stage in stages]
    peers = targets + [peer for line in lines for peer in line]
    barrier = pltpu.get_barrier_semaphore()
    for peer in peers:
        pl.semaphore_signal(barrier, inc=1, device_id=peer, device_id_type=MESH_ID)
    count = count_ref[0]

    loads[0].wait()
    coords = to_rows(nodes_ref, 3, stage_ref)
    for c in range(3):
        v_ref[c] = coords[c]
    loads[1].wait()
    for k in range(BLK):
        lanes = pl.ds(k * LANE, LANE)
        ends_ref[0, k : k + 1, :] = links_ref[0:1, lanes]
        ends_ref[1, k : k + 1, :] = links_ref[1:2, lanes]
    first, second = gather_ends(v_ref, [ends_ref[0], ends_ref[1]])
    loads[2].wait()
    rows = [0.5 * (first[c] + second[c]) for c in range(3)] + [second[c] - first[c] for c in range(3)]
    rows = rows + to_rows(burgers_ref, 3, stage_ref)
    for c in range(9):
        own_ref[c] = rows[c]
        for k in range(BLK):
            block_ref[k, c : c + 1, :] = rows[c][k : k + 1]
    pack_blocks(send_list, block_ref, 9, send_ref)
    pl.semaphore_wait(barrier, len(peers))
    copies = ghost_copies(send_ref, recv_ref, gs1, gr1, targets)
    for copy in copies:
        copy.start()
    loads[3].wait()
    for r in range(3):
        rows = to_rows(mobility_ref, 3, stage_ref, r)
        for c in range(3):
            mob_ref[3 * r + c] = rows[c]

    def fill_first():
        for copy in copies:
            copy.wait_recv()
        for c in range(9):
            for k in range(8):
                ghost_ref[c, 8 * k : 8 * k + GB, :] = recv_ref[k, pl.ds(c, GB, stride=9), :]
                ghost_ref[c, 8 * k + GB : 8 * k + 8, :] = jnp.zeros((8 - GB, LANE), F32)

    def ghost(c, half):
        return ghost_ref[c, BLK * half : BLK * (half + 1), :]

    own = [own_ref[c] for c in range(9)]
    speed = velocity(own, fill_first, ghost, pairs, pair_row, count, ends_ref, mob_ref, scr)
    best = jnp.max(dot3(speed, speed), axis=0, keepdims=True)
    waiting = []

    def spread(stage, value):
        base = sum(len(line) for line in lines[:stage])
        mid_ref[stage] = value
        sent = [
            remote(mid_ref.at[stage], box_ref.at[base + o], ms.at[base + o], mr.at[base + o], peer)
            for o, peer in enumerate(lines[stage])
        ]
        for copy in sent:
            copy.start()
        waiting.extend(sent)
        return base, sent

    def settle(state, value):
        base, sent = state
        for copy in sent:
            copy.wait_recv()
        for o in range(len(sent)):
            value = jnp.maximum(value, box_ref[base + o])
        return value

    state = spread(0, best)
    for c in range(3):
        v_ref[c] = speed[c]
    best = settle(state, best)
    state = spread(1, best)
    first, second = gather_ends(v_ref, [ends_ref[0], ends_ref[1]])
    rows = [0.5 * (first[c] + second[c]) for c in range(3)] + [second[c] - first[c] for c in range(3)]
    for c in range(6):
        own_v_ref[c] = rows[c]
        for k in range(BLK):
            block_ref[k, c : c + 1, :] = rows[c][k : k + 1]
    pack_blocks(send_list, block_ref, 6, send_v_ref)
    copies_v = ghost_copies(send_v_ref, recv_v_ref, gs2, gr2, targets)
    for copy in copies_v:
        copy.start()
    best = settle(state, best)
    state = spread(2, best)
    best = settle(state, best)
    step = DX_LIMIT / (jnp.sqrt(jnp.max(best)) + SPEED_EPS)

    def fill_second():
        for copy in copies_v:
            copy.wait_recv()
        for c in range(6):
            for k in range(8):
                rows = slice(8 * k, 8 * k + GB)
                ghost_ref[c, rows, :] = ghost_ref[c, rows, :] + step * recv_v_ref[k, pl.ds(c, GB, stride=6), :]

    own = [own_ref[c] + step * own_v_ref[c] if c < 6 else own_ref[c] for c in range(9)]
    speed = velocity(own, fill_second, ghost, pairs, pair_row, count, ends_ref, mob_ref, scr)
    for c in range(3):
        stage_ref[pl.ds(c, BLK, stride=8), :] = 0.5 * step * (v_ref[c] + speed[c])
    for k in range(BLK):
        out_ref[:, pl.ds(k * LANE, LANE)] = stage_ref[8 * k : 8 * k + 3, :]
    for copy in copies + copies_v + waiting:
        copy.wait_send()


VMEM = pl.BlockSpec(memory_space=pltpu.VMEM)
SMEM = pl.BlockSpec(memory_space=pltpu.SMEM)
ANY = pl.BlockSpec(memory_space=pl.ANY)
DMA = pltpu.SemaphoreType.DMA


def local(nodes, links, burgers, mobility, send_list, pair_list, pair_count):
    n_gx = lax.axis_size("gx")
    n_yz = lax.axis_size("yz")
    stages = STAGES
    mail = sum(math.prod(size for _, _, size in stage) - 1 for stage in stages)
    scratch = [
        pltpu.VMEM((3, BLK * LANE), F32),
        pltpu.VMEM((2, BLK * LANE), jnp.int32),
        pltpu.VMEM((3, BLK * LANE), F32),
        pltpu.VMEM((3, 3, BLK * LANE), F32),
        DMA((4,)),
        pltpu.VMEM((9, BLK, LANE), F32),
        pltpu.VMEM((6, BLK, LANE), F32),
        pltpu.VMEM((3, BLK, LANE), F32),
        pltpu.VMEM((2, BLK, LANE), jnp.int32),
        pltpu.VMEM((9, BLK, LANE), F32),
        pltpu.VMEM((9, 64, LANE), F32),
        pltpu.VMEM((BLK * 8, LANE), F32),
        pltpu.VMEM((BLK, 16, LANE), F32),
        pltpu.VMEM((8, 9 * GB, LANE), F32),
        pltpu.VMEM((8, 9 * GB, LANE), F32),
        pltpu.VMEM((8, 6 * GB, LANE), F32),
        pltpu.VMEM((8, 6 * GB, LANE), F32),
        pltpu.VMEM((mail, 1, LANE), F32),
        pltpu.VMEM((len(stages), 1, LANE), F32),
        DMA((8,)), DMA((8,)), DMA((8,)), DMA((8,)), DMA((mail,)), DMA((mail,)),
        pltpu.VMEM((SLOTS * QROWS, LANE), F32),
        pltpu.VMEM((BLK * QROWS, LANE), F32),
        pltpu.VMEM((SLOTS * FROWS, LANE), F32),
        pltpu.VMEM((SLOTS, LANE, QROWS), BF16),
        pltpu.VMEM((BLK, QROWS, LANE), BF16),
        pltpu.VMEM((SLOTS, FROWS, 2 * LANE), BF16),
        pltpu.VMEM((24, PAIRS, LANE), F32),
        pltpu.VMEM((6, BLK, LANE), F32),
    ]
    return pl.pallas_call(
        functools.partial(step_kernel, stages),
        out_shape=jax.ShapeDtypeStruct((3, BLK * LANE), F32),
        in_specs=[SMEM, SMEM, SMEM, VMEM, ANY, ANY, ANY, ANY],
        out_specs=VMEM,
        scratch_shapes=scratch,
        compiler_params=pltpu.CompilerParams(collective_id=0, has_side_effects=True, vmem_limit_bytes=56 * 1024 * 1024),
        name="step",
    )(jnp.transpose(send_list, (2, 0, 1)), pair_list, pair_count, pair_list, nodes, links, burgers, mobility)


def solution(mesh):
    return jax.shard_map(
        local,
        mesh=mesh,
        in_specs=(
            P(None, ("gx", "yz")),
            P(None, ("gx", "yz")),
            P(None, ("gx", "yz")),
            P(None, None, ("gx", "yz")),
            P(("gx", "yz"), None, None),
            P(None, ("gx", "yz")),
            P(("gx", "yz")),
        ),
        out_specs=P(None, ("gx", "yz")),
        check_vma=False,
    )
```

time: 102 us -> 69.3 us (0.68)
  the two profiles are of different devices: /device:TPU:32 before, /device:TPU:1 now
where the time goes in v2:
time: 69.3 us; the launch traced here: 69.1 us
  Pallas kernels  67 us (97%)
  local copies, waits for them, and re-layouts  1.48 us (2%)
    pallas_call x1, Pallas kernels, local(): pl.pallas_call(functools.partial(step_kernel, stages), out_shape=jax.Shap...  67 us
    unnamed x1, local copies, waits for them, and re-layouts  1.48 us

profile of v2, /device:TPU:1, one launch (start us, length us, event | category | flops | bytes accessed | tf_op | source)
XLA Modules:
  0.0 69.1 jit_solution(16438464415820556077)
XLA Ops:
  0.7 67.0 %step.1 = f32[3,4096]{1,0:T(4,128)} custom-call(s32[6,1,8]{2,1,0:T(1,128)} %bitcast.1, s32[2,160]{1,0:T(2,128)} %pair_row.1, s32[1]{0:T(128)S(6)} %copy.9.count_ref, s32[2,160]{1,0:T(2,128)} %pair_row.1, f32[3,4096]{1,0:T(4,128)} %nodes_hbm.1, s32[2,4096]{1,0:T(2,128)} %links_hbm.1, f32[3,4096]{1,0:T(4,128)} %burgers_hbm.1, f32[3,3,4096]{2,1,0:T(4,128)} %mobility_hbm.1), custom_call_target="tpu_custom_call" | custom-call | tf_op jit(solution)/shard_map/step/pallas_call | solution.py:448
  67.6 1.5 %copy.10 = f32[3,4096]{1,0:T(4,128)} copy(f32[3,4096]{1,0:T(4,128)} %step.1) | data formatting | bytes 98304

commit v3 on v2

--- a/solution.py
+++ b/solution.py
@@ -20,10 +20,12 @@
 LANE = 128
 GB = 6
 SLOTS = BLK + 64
-QROWS = 32
-FROWS = 48
-UNROLL = 16
-SCAT = 8
+QRAW = 8
+FRAW = 24
+CONV = 8
+QK = 6 * QRAW
+UNROLL = 32
+SCAT = 16
 PAIRS = 160
 MESH_ID = pl.DeviceIdType.MESH
 STAGES = ((("yz", 1, 2),), (("gx", 1, 4), ("yz", 2, 4)), (("gx", 4, 4), ("yz", 8, 4)))
@@ -115,95 +117,97 @@
     return [remote(send_ref.at[k], recv_ref.at[k], send_sem.at[k], recv_sem.at[k], targets[k]) for k in range(8)]
 
 
-def source_features(mid, line, burg, slot, qs_ref, f_ref):
-    def put_q(row, value):
-        qs_ref[pl.ds(slot * QROWS + row, BLK, stride=QROWS), :] = value
-
-    def put_f(row, value):
-        f_ref[pl.ds(slot * FROWS + row, BLK, stride=FROWS), :] = value
-
-    row = 0
-    for c in range(3):
-        high, middle, low = split3(mid[c])
-        for part in (high, high, middle, middle, high, low):
-            put_q(row, part)
-            row += 1
-    for part in split3(dot3(mid, mid) + A_SQUARED):
-        put_q(row, part)
-        row += 1
-    one = jnp.ones((BLK, LANE), F32)
-    zero = jnp.zeros((BLK, LANE), F32)
-    for _ in range(3):
-        put_q(row, one)
-        row += 1
-    while row < QROWS:
-        put_q(row, zero)
-        row += 1
+def put_rows(ref, slot, height, values):
+    for row, value in enumerate(values):
+        if value is not None:
+            ref[pl.ds(slot * height + row, BLK, stride=height), :] = value
+
+
+def filled(value):
+    return jnp.full((BLK, LANE), value, F32)
+
+
+def spread_features(order, slot, mid, line, burg, slope, q_refs, f_refs):
     moment = cross(burg, mid)
-    for a in range(3):
-        for d in range(3):
-            high, low = split2(line[a] * burg[d])
-            put_f(3 * a + d, high)
-            put_f(24 + 3 * a + d, low)
-            high, low = split2(line[a] * moment[d])
-            put_f(9 + 3 * a + d, high)
-            put_f(33 + 3 * a + d, low)
-
-
-def target_features(mid, qt_ref):
-    def put(row, value):
-        qt_ref[pl.ds(row, BLK, stride=QROWS), :] = value
-
-    row = 0
-    for c in range(3):
-        high, middle, low = split3(-2.0 * mid[c])
-        for part in (high, middle, high, middle, low, high):
-            put(row, part)
-            row += 1
-    one = jnp.ones((BLK, LANE), F32)
-    zero = jnp.zeros((BLK, LANE), F32)
-    for _ in range(3):
-        put(row, one)
-        row += 1
-    for part in split3(dot3(mid, mid)):
-        put(row, part)
-        row += 1
-    while row < QROWS:
-        put(row, zero)
-        row += 1
-
-
-def velocity(own, fill_ghost, ghost, pairs, pair_row, count, ends_ref, mob_ref, scr):
-    qs_f, qt_f, f_f, qs_b, qt_b, f_b, acc, force_ref = scr
-    centre = [jnp.mean(own[c]) for c in range(3)]
-    mid = [own[c] - centre[c] for c in range(3)]
-    line = own[3:6]
-    burg = own[6:9]
-    source_features(mid, line, burg, 0, qs_f, f_f)
-    target_features(mid, qt_f)
-    fill_ghost()
-    for half in range(2):
-        rows = [ghost(c, half) for c in range(9)]
-        source_features([rows[c] - centre[c] for c in range(3)], rows[3:6], rows[6:9], BLK * (half + 1), qs_f, f_f)
-
-    def convert(step, carry):
-        for j in range(4):
-            slot = 4 * step + j
-            q = qs_f[pl.ds(pl.multiple_of(slot * QROWS, 8), QROWS), :]
-            qs_b[slot] = jnp.transpose(q).astype(BF16)
-            f = f_f[pl.ds(pl.multiple_of(slot * FROWS, 8), FROWS), :].astype(BF16)
-            f_b[slot] = jnp.concatenate([f, f], axis=1)
+    if order == 0:
+        put_rows(q_refs[0], slot, QRAW, mid + [dot3(mid, mid) + A_SQUARED, filled(1.0)] + [filled(0.0)] * 3)
+        put_rows(f_refs[0], slot, FRAW, [line[a] * burg[d] for a in range(3) for d in range(3)])
+        put_rows(f_refs[0], slot, FRAW, [None] * 9 + [line[a] * moment[d] for a in range(3) for d in range(3)])
+        return
+    mid_v, line_v = slope
+    moment_v = cross(burg, mid_v)
+    put_rows(q_refs[1], slot, QRAW, mid_v + [2.0 * dot3(mid, mid_v), dot3(mid_v, mid_v)] + [filled(0.0)] * 3)
+    put_rows(f_refs[1], slot, FRAW, [line_v[a] * burg[d] for a in range(3) for d in range(3)])
+    put_rows(
+        f_refs[1], slot, FRAW,
+        [None] * 9 + [line[a] * moment_v[d] + line_v[a] * moment[d] for a in range(3) for d in range(3)],
+    )
+    put_rows(f_refs[2], slot, FRAW, [filled(0.0)] * 9 + [line_v[a] * moment_v[d] for a in range(3) for d in range(3)])
+
+
+def over_slots(own, ghosts, body):
+    def own_trip(trip, carry):
+        for j in range(CONV):
+            body(CONV * trip + j)
         return carry
 
-    lax.fori_loop(0, SLOTS // 4, convert, 0)
-
-    def convert_target(step, carry):
-        for j in range(4):
-            slot = 4 * step + j
-            qt_b[slot] = qt_f[pl.ds(pl.multiple_of(slot * QROWS, 8), QROWS), :].astype(BF16)
+    def ghost_trip(trip, carry):
+        for j in range(GB):
+            body(BLK + 8 * trip + j)
         return carry
 
-    lax.fori_loop(0, BLK // 4, convert_target, 0)
+    if own:
+        lax.fori_loop(0, BLK // CONV, own_trip, 0)
+    if ghosts:
+        lax.fori_loop(0, 8, ghost_trip, 0)
+
+
+def turn_sources(order, own, ghosts, q_refs, qs_b):
+    def body(slot):
+        rows = pl.ds(pl.multiple_of(slot * QRAW, 8), QRAW)
+        high, mid, low = split3(q_refs[order][rows, :])
+        turned = jnp.transpose(jnp.concatenate([high, high, mid, mid, high, low], axis=0)).astype(BF16)
+        qs_b[slot, :, QK * order : QK * (order + 1)] = turned
+
+    over_slots(own, ghosts, body)
+
+
+def convert_features(own, ghosts, step, f_refs, f_b):
+    def body(slot):
+        rows = pl.ds(pl.multiple_of(slot * FRAW, 8), FRAW)
+        value = f_refs[0][rows, :]
+        if step is not None:
+            value = value + step * (f_refs[1][rows, :] + step * f_refs[2][rows, :])
+        high, low = split2(value)
+        part = jnp.concatenate([high, low], axis=0).astype(BF16)
+        f_b[slot, :, 0:LANE] = part
+        f_b[slot, :, LANE : 2 * LANE] = part
+
+    over_slots(own, ghosts, body)
+
+
+def convert_targets(mid, step, t_refs, qt_b):
+    put_rows(t_refs[0], 0, QRAW, [-2.0 * mid[c] for c in range(3)] + [filled(1.0), dot3(mid, mid)] + [filled(0.0)] * 3)
+    orders = 1
+    if step is not None:
+        orders = 2
+        flat = filled(1.0) * step
+        put_rows(t_refs[1], 0, QRAW, [-2.0 * step * mid[c] for c in range(3)] + [flat, step * flat] + [filled(0.0)] * 3)
+
+    def body(trip, carry):
+        for j in range(CONV):
+            slot = CONV * trip + j
+            for order in range(orders):
+                high, mid_part, low = split3(t_refs[order][pl.ds(pl.multiple_of(slot * QRAW, 8), QRAW), :])
+                qt_b[slot, QK * order : QK * (order + 1), :] = jnp.concatenate(
+                    [high, mid_part, high, mid_part, low, high], axis=0
+                ).astype(BF16)
+        return carry
+
+    lax.fori_loop(0, BLK // CONV, body, 0)
+
+
+def pair_sums(depth, mid, line, burg, pairs, pair_row, count, ends_ref, mob_ref, qs_b, qt_b, f_b, acc, force_ref):
     def pair_step(step, carry):
         for j in range(UNROLL):
             place = UNROLL * step + j
@@ -212,14 +216,14 @@
             ghost_place = source - BLK
             group = (ghost_place * 43) >> 8
             slot = jnp.where(source < BLK, source, BLK + 8 * group + (ghost_place - GB * group))
-            dist = jnp.dot(qs_b[slot], qt_b[target], preferred_element_type=F32)
+            dist = jnp.dot(qs_b[slot, :, 0:depth], qt_b[target, 0:depth, :], preferred_element_type=F32)
             root = lax.rsqrt(dist)
             weight = root * root * root
             high = weight.astype(BF16)
             low = (weight - high.astype(F32)).astype(BF16)
             both = jnp.concatenate([high, low], axis=0)
             found = jnp.dot(f_b[slot], both, preferred_element_type=F32)
-            acc[:, place, :] = found[0:24] + found[24:48]
+            acc[:, place, :] = found[0:FRAW] + found[FRAW : 2 * FRAW]
         return carry
 
     lax.fori_loop(0, PAIRS // UNROLL, pair_step, 0)
@@ -283,8 +287,9 @@
 def step_kernel(
     stages, send_list, pairs, count_ref, pair_row, nodes_hbm, links_hbm, burgers_hbm, mobility_hbm, out_ref,
     nodes_ref, links_ref, burgers_ref, mobility_ref, in_sem,
-    own_ref, own_v_ref, v_ref, ends_ref, mob_ref, ghost_ref, stage_ref, block_ref,
-    send_ref, recv_ref, send_v_ref, recv_v_ref, box_ref, mid_ref, gs1, gr1, gs2, gr2, ms, mr, *scr
+    own_ref, own_v_ref, v_ref, ends_ref, mob_ref, ghost_ref, ghost_v_ref, stage_ref, block_ref,
+    send_ref, recv_ref, send_v_ref, recv_v_ref, box_ref, mid_ref, gs1, gr1, gs2, gr2, ms, mr,
+    q0_ref, q1_ref, f0_ref, f1_ref, f2_ref, t0_ref, t1_ref, qs_b, qt_b, f_b, acc, force_ref
 ):
     loads = [
         pltpu.make_async_copy(src, dst, in_sem.at[i])
@@ -330,19 +335,35 @@
         for c in range(3):
             mob_ref[3 * r + c] = rows[c]
 
-    def fill_first():
-        for copy in copies:
-            copy.wait_recv()
-        for c in range(9):
-            for k in range(8):
-                ghost_ref[c, 8 * k : 8 * k + GB, :] = recv_ref[k, pl.ds(c, GB, stride=9), :]
-                ghost_ref[c, 8 * k + GB : 8 * k + 8, :] = jnp.zeros((8 - GB, LANE), F32)
-
-    def ghost(c, half):
-        return ghost_ref[c, BLK * half : BLK * (half + 1), :]
-
+    q_refs = (q0_ref, q1_ref)
+    t_refs = (t0_ref, t1_ref)
+    f_refs = (f0_ref, f1_ref, f2_ref)
+    tables = (qs_b, qt_b, f_b, acc, force_ref)
     own = [own_ref[c] for c in range(9)]
-    speed = velocity(own, fill_first, ghost, pairs, pair_row, count, ends_ref, mob_ref, scr)
+    centre = [jnp.mean(own[c]) for c in range(3)]
+    mid = [own[c] - centre[c] for c in range(3)]
+    spread_features(0, 0, mid, own[3:6], own[6:9], None, q_refs, f_refs)
+    turn_sources(0, True, False, q_refs, qs_b)
+    convert_features(True, False, None, f_refs, f_b)
+    convert_targets(mid, None, t_refs, qt_b)
+    for copy in copies:
+        copy.wait_recv()
+    for c in range(9):
+        for k in range(8):
+            ghost_ref[c, 8 * k : 8 * k + GB, :] = recv_ref[k, pl.ds(c, GB, stride=9), :]
+            ghost_ref[c, 8 * k + GB : 8 * k + 8, :] = jnp.zeros((8 - GB, LANE), F32)
+            if c < 6:
+                ghost_v_ref[c, 8 * k + GB : 8 * k + 8, :] = jnp.zeros((8 - GB, LANE), F32)
+
+    def ghost(half):
+        rows = [ghost_ref[c, BLK * half : BLK * (half + 1), :] for c in range(9)]
+        return [rows[c] - centre[c] for c in range(3)], rows[3:6], rows[6:9]
+
+    for half in range(2):
+        spread_features(0, BLK * (half + 1), *ghost(half), None, q_refs, f_refs)
+    turn_sources(0, False, True, q_refs, qs_b)
+    convert_features(False, True, None, f_refs, f_b)
+    speed = pair_sums(QK, mid, own[3:6], own[6:9], pairs, pair_row, count, ends_ref, mob_ref, *tables)
     best = jnp.max(dot3(speed, speed), axis=0, keepdims=True)
     waiting = []
 
@@ -383,19 +404,27 @@
         copy.start()
     best = settle(state, best)
     state = spread(2, best)
+    own = [own_ref[c] for c in range(9)]
+    mid = [own[c] - centre[c] for c in range(3)]
+    own_v = [own_v_ref[c] for c in range(6)]
+    spread_features(1, 0, mid, own[3:6], own[6:9], (own_v[0:3], own_v[3:6]), q_refs, f_refs)
+    turn_sources(1, True, False, q_refs, qs_b)
+    for copy in copies_v:
+        copy.wait_recv()
+    for c in range(6):
+        for k in range(8):
+            ghost_v_ref[c, 8 * k : 8 * k + GB, :] = recv_v_ref[k, pl.ds(c, GB, stride=6), :]
+    for half in range(2):
+        moving = [ghost_v_ref[c, BLK * half : BLK * (half + 1), :] for c in range(6)]
+        spread_features(1, BLK * (half + 1), *ghost(half), (moving[0:3], moving[3:6]), q_refs, f_refs)
+    turn_sources(1, False, True, q_refs, qs_b)
     best = settle(state, best)
     step = DX_LIMIT / (jnp.sqrt(jnp.max(best)) + SPEED_EPS)
-
-    def fill_second():
-        for copy in copies_v:
-            copy.wait_recv()
-        for c in range(6):
-            for k in range(8):
-                rows = slice(8 * k, 8 * k + GB)
-                ghost_ref[c, rows, :] = ghost_ref[c, rows, :] + step * recv_v_ref[k, pl.ds(c, GB, stride=6), :]
-
-    own = [own_ref[c] + step * own_v_ref[c] if c < 6 else own_ref[c] for c in range(9)]
-    speed = velocity(own, fill_second, ghost, pairs, pair_row, count, ends_ref, mob_ref, scr)
+    convert_features(True, True, step, f_refs, f_b)
+    mid = [mid[c] + step * own_v[c] for c in range(3)]
+    line = [own[3 + c] + step * own_v[3 + c] for c in range(3)]
+    convert_targets(mid, step, t_refs, qt_b)
+    speed = pair_sums(2 * QK, mid, line, own[6:9], pairs, pair_row, count, ends_ref, mob_ref, *tables)
     for c in range(3):
         stage_ref[pl.ds(c, BLK, stride=8), :] = 0.5 * step * (v_ref[c] + speed[c])
     for k in range(BLK):
@@ -427,6 +456,7 @@
         pltpu.VMEM((2, BLK, LANE), jnp.int32),
         pltpu.VMEM((9, BLK, LANE), F32),
         pltpu.VMEM((9, 64, LANE), F32),
+        pltpu.VMEM((6, 64, LANE), F32),
         pltpu.VMEM((BLK * 8, LANE), F32),
         pltpu.VMEM((BLK, 16, LANE), F32),
         pltpu.VMEM((8, 9 * GB, LANE), F32),
@@ -436,13 +466,13 @@
         pltpu.VMEM((mail, 1, LANE), F32),
         pltpu.VMEM((len(stages), 1, LANE), F32),
         DMA((8,)), DMA((8,)), DMA((8,)), DMA((8,)), DMA((mail,)), DMA((mail,)),
-        pltpu.VMEM((SLOTS * QROWS, LANE), F32),
-        pltpu.VMEM((BLK * QROWS, LANE), F32),
-        pltpu.VMEM((SLOTS * FROWS, LANE), F32),
-        pltpu.VMEM((SLOTS, LANE, QROWS), BF16),
-        pltpu.VMEM((BLK, QROWS, LANE), BF16),
-        pltpu.VMEM((SLOTS, FROWS, 2 * LANE), BF16),
-        pltpu.VMEM((24, PAIRS, LANE), F32),
+        *[pltpu.VMEM((SLOTS * QRAW, LANE), F32)] * 2,
+        *[pltpu.VMEM((SLOTS * FRAW, LANE), F32)] * 3,
+        *[pltpu.VMEM((BLK * QRAW, LANE), F32)] * 2,
+        pltpu.VMEM((SLOTS, LANE, 2 * QK), BF16),
+        pltpu.VMEM((BLK, 2 * QK, LANE), BF16),
+        pltpu.VMEM((SLOTS, 2 * FRAW, 2 * LANE), BF16),
+        pltpu.VMEM((FRAW, PAIRS, LANE), F32),
         pltpu.VMEM((6, BLK, LANE), F32),
     ]
     return pl.pallas_call(

time: 69.3 us -> 59.6 us (0.86); the launches traced: 69.1 us -> 58.7 us
  Pallas kernels: 67 us -> 56.6 us
    pallas_call x1, Pallas kernels: 67 us -> 56.6 us  [local(): pl.pallas_call(functools.partial(step_kernel, stages), out_shape=jax.Shap...]
where the time goes in v3:
time: 59.6 us; the launch traced here: 58.7 us
  Pallas kernels  56.6 us (95%)
  local copies, waits for them, and re-layouts  1.48 us (2%)
  between operations  0.66 us (1%)
    pallas_call x1, Pallas kernels, local(): pl.pallas_call(functools.partial(step_kernel, stages), out_shape=jax.Shap...  56.6 us
    unnamed x1, local copies, waits for them, and re-layouts  1.48 us

profile of v3, /device:TPU:1, one launch (start us, length us, event | category | flops | bytes accessed | tf_op | source)
XLA Modules:
  0.0 58.7 jit_solution(15311499268796366495)
XLA Ops:
  0.7 56.6 %step.1 = f32[3,4096]{1,0:T(4,128)} custom-call(s32[6,1,8]{2,1,0:T(1,128)} %bitcast.1, s32[2,160]{1,0:T(2,128)} %pair_row.1, s32[1]{0:T(128)S(6)} %copy.9.count_ref, s32[2,160]{1,0:T(2,128)} %pair_row.1, f32[3,4096]{1,0:T(4,128)} %nodes_hbm.1, s32[2,4096]{1,0:T(2,128)} %links_hbm.1, f32[3,4096]{1,0:T(4,128)} %burgers_hbm.1, f32[3,3,4096]{2,1,0:T(4,128)} %mobility_hbm.1), custom_call_target="tpu_custom_call" | custom-call | tf_op jit(solution)/shard_map/step/pallas_call | solution.py:478
  57.2 1.5 %copy.10 = f32[3,4096]{1,0:T(4,128)} copy(f32[3,4096]{1,0:T(4,128)} %step.1) | data formatting | bytes 98304

commit v4 on v3

--- a/solution.py
+++ b/solution.py
@@ -22,11 +22,12 @@
 SLOTS = BLK + 64
 QRAW = 8
 FRAW = 24
-CONV = 8
+CONV = 16
 QK = 6 * QRAW
-UNROLL = 32
+UNROLL = 40
 SCAT = 16
 PAIRS = 160
+PSTRIDE = PAIRS + 8
 MESH_ID = pl.DeviceIdType.MESH
 STAGES = ((("yz", 1, 2),), (("gx", 1, 4), ("yz", 2, 4)), (("gx", 4, 4), ("yz", 8, 4)))
 
@@ -223,7 +224,7 @@
             low = (weight - high.astype(F32)).astype(BF16)
             both = jnp.concatenate([high, low], axis=0)
             found = jnp.dot(f_b[slot], both, preferred_element_type=F32)
-            acc[:, place, :] = found[0:FRAW] + found[FRAW : 2 * FRAW]
+            acc[pl.ds(place, FRAW, stride=PSTRIDE), :] = found[0:FRAW] + found[FRAW : 2 * FRAW]
         return carry
 
     lax.fori_loop(0, PAIRS // UNROLL, pair_step, 0)
@@ -233,8 +234,9 @@
     chosen = jnp.concatenate([chosen, chosen], axis=1)
 
     def total(row):
-        high = acc[row].astype(BF16)
-        low = (acc[row] - high.astype(F32)).astype(BF16)
+        part = acc[PSTRIDE * row : PSTRIDE * row + PAIRS, :]
+        high = part.astype(BF16)
+        low = (part - high.astype(F32)).astype(BF16)
         return jnp.dot(chosen, jnp.concatenate([high, low], axis=0), preferred_element_type=F32)
 
     s_mat = [[total(3 * a + d) for d in range(3)] for a in range(3)]
@@ -285,8 +287,8 @@
 
 
 def step_kernel(
-    stages, send_list, pairs, count_ref, pair_row, nodes_hbm, links_hbm, burgers_hbm, mobility_hbm, out_ref,
-    nodes_ref, links_ref, burgers_ref, mobility_ref, in_sem,
+    stages, send_list_hbm, pairs_hbm, count_hbm, nodes_hbm, links_hbm, burgers_hbm, mobility_hbm, out_ref,
+    nodes_ref, links_ref, burgers_ref, mobility_ref, send_list, pairs, count_ref, pair_row, in_sem,
     own_ref, own_v_ref, v_ref, ends_ref, mob_ref, ghost_ref, ghost_v_ref, stage_ref, block_ref,
     send_ref, recv_ref, send_v_ref, recv_v_ref, box_ref, mid_ref, gs1, gr1, gs2, gr2, ms, mr,
     q0_ref, q1_ref, f0_ref, f1_ref, f2_ref, t0_ref, t1_ref, qs_b, qt_b, f_b, acc, force_ref
@@ -294,7 +296,16 @@
     loads = [
         pltpu.make_async_copy(src, dst, in_sem.at[i])
         for i, (src, dst) in enumerate(
-            ((nodes_hbm, nodes_ref), (links_hbm, links_ref), (burgers_hbm, burgers_ref), (mobility_hbm, mobility_ref))
+            (
+                (nodes_hbm, nodes_ref),
+                (links_hbm, links_ref),
+                (burgers_hbm, burgers_ref),
+                (send_list_hbm, send_list),
+                (mobility_hbm, mobility_ref),
+                (pairs_hbm, pairs),
+                (pairs_hbm, pair_row),
+                (count_hbm, count_ref),
+            )
         )
     ]
     for load in loads:
@@ -305,7 +316,6 @@
     barrier = pltpu.get_barrier_semaphore()
     for peer in peers:
         pl.semaphore_signal(barrier, inc=1, device_id=peer, device_id_type=MESH_ID)
-    count = count_ref[0]
 
     loads[0].wait()
     coords = to_rows(nodes_ref, 3, stage_ref)
@@ -324,12 +334,15 @@
         own_ref[c] = rows[c]
         for k in range(BLK):
             block_ref[k, c : c + 1, :] = rows[c][k : k + 1]
+    loads[3].wait()
     pack_blocks(send_list, block_ref, 9, send_ref)
     pl.semaphore_wait(barrier, len(peers))
     copies = ghost_copies(send_ref, recv_ref, gs1, gr1, targets)
     for copy in copies:
         copy.start()
-    loads[3].wait()
+    for load in loads[4:]:
+        load.wait()
+    count = count_ref[0]
     for r in range(3):
         rows = to_rows(mobility_ref, 3, stage_ref, r)
         for c in range(3):
@@ -434,8 +447,7 @@
 
 
 VMEM = pl.BlockSpec(memory_space=pltpu.VMEM)
-SMEM = pl.BlockSpec(memory_space=pltpu.SMEM)
-ANY = pl.BlockSpec(memory_space=pl.ANY)
+HBM = pl.BlockSpec(memory_space=pltpu.HBM)
 DMA = pltpu.SemaphoreType.DMA
 
 
@@ -449,7 +461,11 @@
         pltpu.VMEM((2, BLK * LANE), jnp.int32),
         pltpu.VMEM((3, BLK * LANE), F32),
         pltpu.VMEM((3, 3, BLK * LANE), F32),
-        DMA((4,)),
+        pltpu.SMEM((GB, 1, 8), jnp.int32),
+        pltpu.SMEM((2, PAIRS), jnp.int32),
+        pltpu.SMEM((1,), jnp.int32),
+        pltpu.VMEM((2, PAIRS), jnp.int32),
+        DMA((8,)),
         pltpu.VMEM((9, BLK, LANE), F32),
         pltpu.VMEM((6, BLK, LANE), F32),
         pltpu.VMEM((3, BLK, LANE), F32),
@@ -472,18 +488,18 @@
         pltpu.VMEM((SLOTS, LANE, 2 * QK), BF16),
         pltpu.VMEM((BLK, 2 * QK, LANE), BF16),
         pltpu.VMEM((SLOTS, 2 * FRAW, 2 * LANE), BF16),
-        pltpu.VMEM((FRAW, PAIRS, LANE), F32),
+        pltpu.VMEM((FRAW * PSTRIDE, LANE), F32),
         pltpu.VMEM((6, BLK, LANE), F32),
     ]
     return pl.pallas_call(
         functools.partial(step_kernel, stages),
         out_shape=jax.ShapeDtypeStruct((3, BLK * LANE), F32),
-        in_specs=[SMEM, SMEM, SMEM, VMEM, ANY, ANY, ANY, ANY],
+        in_specs=[HBM] * 7,
         out_specs=VMEM,
         scratch_shapes=scratch,
         compiler_params=pltpu.CompilerParams(collective_id=0, has_side_effects=True, vmem_limit_bytes=56 * 1024 * 1024),
         name="step",
-    )(jnp.transpose(send_list, (2, 0, 1)), pair_list, pair_count, pair_list, nodes, links, burgers, mobility)
+    )(jnp.transpose(send_list, (2, 0, 1)), pair_list, pair_count, nodes, links, burgers, mobility)
 
 
 def solution(mesh):

time: 59.6 us -> 56.7 us (0.951)
  Pallas kernels: 56.6 us -> 53.7 us
    pallas_call x1, Pallas kernels: 56.6 us -> 53.7 us  [local(): pl.pallas_call(functools.partial(step_kernel, stages), out_shape=jax.Shap...]
where the time goes in v4:
time: 56.7 us; the launch traced here: 55.9 us
  Pallas kernels  53.7 us (95%)
  local copies, waits for them, and re-layouts  1.48 us (3%)
  between operations  0.66 us (1%)
    pallas_call x1, Pallas kernels, local(): pl.pallas_call(functools.partial(step_kernel, stages), out_shape=jax.Shap...  53.7 us
    unnamed x1, local copies, waits for them, and re-layouts  1.48 us

profile of v4, /device:TPU:1, one launch (start us, length us, event | category | flops | bytes accessed | tf_op | source)
XLA Modules:
  0.0 55.9 jit_solution(357875539292196577)
XLA Ops:
  0.7 53.7 %step.1 = f32[3,4096]{1,0:T(4,128)} custom-call(s32[6,1,8]{2,1,0:T(1,128)} %bitcast.1, s32[2,160]{1,0:T(2,128)} %pairs_hbm.1, s32[1]{0:T(128)S(6)} %copy.9.count_hbm, f32[3,4096]{1,0:T(4,128)} %nodes_hbm.1, s32[2,4096]{1,0:T(2,128)} %links_hbm.1, f32[3,4096]{1,0:T(4,128)} %burgers_hbm.1, f32[3,3,4096]{2,1,0:T(4,128)} %mobility_hbm.1), custom_call_target="tpu_custom_call" | custom-call | tf_op jit(solution)/shard_map/step/pallas_call | solution.py:494
  54.4 1.5 %copy.10 = f32[3,4096]{1,0:T(4,128)} copy(f32[3,4096]{1,0:T(4,128)} %step.1) | data formatting | bytes 98304

commit v5 on v4

--- a/solution.py
+++ b/solution.py
@@ -24,7 +24,7 @@
 FRAW = 24
 CONV = 16
 QK = 6 * QRAW
-UNROLL = 40
+UNROLL = 80
 SCAT = 16
 PAIRS = 160
 PSTRIDE = PAIRS + 8
@@ -493,7 +493,7 @@
     ]
     return pl.pallas_call(
         functools.partial(step_kernel, stages),
-        out_shape=jax.ShapeDtypeStruct((3, BLK * LANE), F32),
+        out_shape=pltpu.VMEM((3, BLK * LANE), F32),
         in_specs=[HBM] * 7,
         out_specs=VMEM,
         scratch_shapes=scratch,

time: 56.7 us -> 54.1 us (0.954)
  Pallas kernels: 53.7 us -> 52 us
  local copies, waits for them, and re-layouts: 1.48 us -> 0.63 us
    pallas_call x1, Pallas kernels: 53.7 us -> 52 us  [local(): pl.pallas_call(functools.partial(step_kernel, stages), out_shape=pltpu.VM...]
    unnamed x1, local copies, waits for them, and re-layouts: 1.48 us -> 0.63 us
where the time goes in v5:
time: 54.1 us; the launch traced here: 53.3 us
  Pallas kernels  52 us (96%)
  between operations  0.66 us (1%)
  local copies, waits for them, and re-layouts  0.63 us (1%)
    pallas_call x1, Pallas kernels, local(): pl.pallas_call(functools.partial(step_kernel, stages), out_shape=pltpu.VM...  52 us

profile of v5, /device:TPU:1, one launch (start us, length us, event | category | flops | bytes accessed | tf_op | source)
XLA Modules:
  0.0 53.3 jit_solution(1992186299696052578)
XLA Ops:
  0.7 52.0 %step.1 = f32[3,4096]{1,0:T(4,128)S(1)} custom-call(s32[6,1,8]{2,1,0:T(1,128)} %bitcast.1, s32[2,160]{1,0:T(2,128)} %pairs_hbm.1, s32[1]{0:T(128)S(6)} %copy.10.count_hbm, f32[3,4096]{1,0:T(4,128)} %nodes_hbm.1, s32[2,4096]{1,0:T(2,128)} %links_hbm.1, f32[3,4096]{1,0:T(4,128)} %burgers_hbm.1, f32[3,3,4096]{2,1,0:T(4,128)} %mobility_hbm.1), custom_call_target="tpu_custom_call" | custom-call | tf_op jit(solution)/shard_map/step/pallas_call | solution.py:494
  52.7 0.6 %copy.9 = f32[3,4096]{1,0:T(4,128)} copy(f32[3,4096]{1,0:T(4,128)S(1)} %step.1) | data formatting | bytes 98304

commit v6 on v5

--- a/solution.py
+++ b/solution.py
@@ -22,10 +22,11 @@
 SLOTS = BLK + 64
 QRAW = 8
 FRAW = 24
-CONV = 16
+CONV = 32
+GTRIP = 8
 QK = 6 * QRAW
-UNROLL = 80
-SCAT = 16
+UNROLL = 160
+SCAT = 32
 PAIRS = 160
 PSTRIDE = PAIRS + 8
 MESH_ID = pl.DeviceIdType.MESH
@@ -153,21 +154,22 @@
         return carry
 
     def ghost_trip(trip, carry):
-        for j in range(GB):
-            body(BLK + 8 * trip + j)
+        for j in range(8 * GTRIP):
+            if j % 8 < GB:
+                body(BLK + 8 * GTRIP * trip + j)
         return carry
 
     if own:
         lax.fori_loop(0, BLK // CONV, own_trip, 0)
     if ghosts:
-        lax.fori_loop(0, 8, ghost_trip, 0)
+        lax.fori_loop(0, 8 // GTRIP, ghost_trip, 0)
 
 
 def turn_sources(order, own, ghosts, q_refs, qs_b):
     def body(slot):
         rows = pl.ds(pl.multiple_of(slot * QRAW, 8), QRAW)
         high, mid, low = split3(q_refs[order][rows, :])
-        turned = jnp.transpose(jnp.concatenate([high, high, mid, mid, high, low], axis=0)).astype(BF16)
+        turned = jnp.transpose(jnp.concatenate([high, high, mid, mid, high, low], axis=0).astype(BF16))
         qs_b[slot, :, QK * order : QK * (order + 1)] = turned
 
     over_slots(own, ghosts, body)

time: 54.1 us -> 60.5 us (1.12); the launches traced: 53.3 us -> 60.3 us
  Pallas kernels: 52 us -> 59 us
    pallas_call x1, Pallas kernels: 52 us -> 59 us  [local(): pl.pallas_call(functools.partial(step_kernel, stages), out_shape=pltpu.VM...]
where the time goes in v6:
time: 60.5 us; the launch traced here: 60.3 us
  Pallas kernels  59 us (98%)
  between operations  0.66 us (1%)
  local copies, waits for them, and re-layouts  0.63 us (1%)
    pallas_call x1, Pallas kernels, local(): pl.pallas_call(functools.partial(step_kernel, stages), out_shape=pltpu.VM...  59 us

profile of v6, /device:TPU:1, one launch (start us, length us, event | category | flops | bytes accessed | tf_op | source)
XLA Modules:
  0.0 60.3 jit_solution(9760553122349948158)
XLA Ops:
  0.7 59.0 %step.1 = f32[3,4096]{1,0:T(4,128)S(1)} custom-call(s32[6,1,8]{2,1,0:T(1,128)} %bitcast.1, s32[2,160]{1,0:T(2,128)} %pairs_hbm.1, s32[1]{0:T(128)S(6)} %copy.10.count_hbm, f32[3,4096]{1,0:T(4,128)} %nodes_hbm.1, s32[2,4096]{1,0:T(2,128)} %links_hbm.1, f32[3,4096]{1,0:T(4,128)} %burgers_hbm.1, f32[3,3,4096]{2,1,0:T(4,128)} %mobility_hbm.1), custom_call_target="tpu_custom_call" | custom-call | tf_op jit(solution)/shard_map/step/pallas_call | solution.py:496
  59.7 0.6 %copy.9 = f32[3,4096]{1,0:T(4,128)} copy(f32[3,4096]{1,0:T(4,128)S(1)} %step.1) | data formatting | bytes 98304

commit v7 on v6

--- a/solution.py
+++ b/solution.py
@@ -22,11 +22,11 @@
 SLOTS = BLK + 64
 QRAW = 8
 FRAW = 24
-CONV = 32
-GTRIP = 8
+CONV = 16
+GTRIP = 2
 QK = 6 * QRAW
-UNROLL = 160
-SCAT = 32
+UNROLL = 80
+SCAT = 16
 PAIRS = 160
 PSTRIDE = PAIRS + 8
 MESH_ID = pl.DeviceIdType.MESH

time: 60.5 us -> 53 us (0.88)
  Pallas kernels: 59 us -> 51.5 us
    pallas_call x1, Pallas kernels: 59 us -> 51.5 us  [local(): pl.pallas_call(functools.partial(step_kernel, stages), out_shape=pltpu.VM...]
where the time goes in v7:
time: 53 us; the launch traced here: 52.8 us
  Pallas kernels  51.5 us (97%)
  between operations  0.66 us (1%)
  local copies, waits for them, and re-layouts  0.63 us (1%)
    pallas_call x1, Pallas kernels, local(): pl.pallas_call(functools.partial(step_kernel, stages), out_shape=pltpu.VM...  51.5 us

profile of v7, /device:TPU:1, one launch (start us, length us, event | category | flops | bytes accessed | tf_op | source)
XLA Modules:
  0.0 52.8 jit_solution(7153821058848740209)
XLA Ops:
  0.7 51.5 %step.1 = f32[3,4096]{1,0:T(4,128)S(1)} custom-call(s32[6,1,8]{2,1,0:T(1,128)} %bitcast.1, s32[2,160]{1,0:T(2,128)} %pairs_hbm.1, s32[1]{0:T(128)S(6)} %copy.10.count_hbm, f32[3,4096]{1,0:T(4,128)} %nodes_hbm.1, s32[2,4096]{1,0:T(2,128)} %links_hbm.1, f32[3,4096]{1,0:T(4,128)} %burgers_hbm.1, f32[3,3,4096]{2,1,0:T(4,128)} %mobility_hbm.1), custom_call_target="tpu_custom_call" | custom-call | tf_op jit(solution)/shard_map/step/pallas_call | solution.py:496
  52.2 0.6 %copy.9 = f32[3,4096]{1,0:T(4,128)} copy(f32[3,4096]{1,0:T(4,128)S(1)} %step.1) | data formatting | bytes 98304

commit v8 on v7

--- a/solution.py
+++ b/solution.py
@@ -25,7 +25,7 @@
 CONV = 16
 GTRIP = 2
 QK = 6 * QRAW
-UNROLL = 80
+UNROLL = 40
 SCAT = 16
 PAIRS = 160
 PSTRIDE = PAIRS + 8
@@ -70,13 +70,19 @@
     for end in ends:
         high = end >> 7
         low = end & 127
-        picked = [jnp.zeros((BLK, LANE), F32) for _ in range(3)]
-        for row in range(BLK):
-            here = high == row
-            for c in range(3):
-                wide = jnp.broadcast_to(table_ref[c, row : row + 1, :], (BLK, LANE))
-                found = jnp.take_along_axis(wide, low, axis=1, mode="promise_in_bounds")
-                picked[c] = jnp.where(here, found, picked[c])
+
+        def rows_step(step, picked, high=high, low=low):
+            picked = list(picked)
+            for j in range(8):
+                row = 8 * step + j
+                here = high == row
+                for c in range(3):
+                    wide = jnp.broadcast_to(table_ref[c, pl.ds(row, 1), :], (BLK, LANE))
+                    found = jnp.take_along_axis(wide, low, axis=1, mode="promise_in_bounds")
+                    picked[c] = jnp.where(here, found, picked[c])
+            return tuple(picked)
+
+        picked = lax.fori_loop(0, BLK // 8, rows_step, tuple(jnp.zeros((BLK, LANE), F32) for _ in range(3)))
         outs.append(picked)
     return outs
 

time: 53 us -> 54.9 us (1.036)
  Pallas kernels: 51.5 us -> 53.5 us
    pallas_call x1, Pallas kernels: 51.5 us -> 53.5 us  [local(): pl.pallas_call(functools.partial(step_kernel, stages), out_shape=pltpu.VM...]
where the time goes in v8:
time: 54.9 us; the launch traced here: 54.8 us
  Pallas kernels  53.5 us (97%)
  between operations  0.66 us (1%)
  local copies, waits for them, and re-layouts  0.63 us (1%)
    pallas_call x1, Pallas kernels, local(): pl.pallas_call(functools.partial(step_kernel, stages), out_shape=pltpu.VM...  53.5 us

profile of v8, /device:TPU:1, one launch (start us, length us, event | category | flops | bytes accessed | tf_op | source)
XLA Modules:
  0.0 54.8 jit_solution(2429360789143669274)
XLA Ops:
  0.7 53.5 %step.1 = f32[3,4096]{1,0:T(4,128)S(1)} custom-call(s32[6,1,8]{2,1,0:T(1,128)} %bitcast.1, s32[2,160]{1,0:T(2,128)} %pairs_hbm.1, s32[1]{0:T(128)S(6)} %copy.10.count_hbm, f32[3,4096]{1,0:T(4,128)} %nodes_hbm.1, s32[2,4096]{1,0:T(2,128)} %links_hbm.1, f32[3,4096]{1,0:T(4,128)} %burgers_hbm.1, f32[3,3,4096]{2,1,0:T(4,128)} %mobility_hbm.1), custom_call_target="tpu_custom_call" | custom-call | tf_op jit(solution)/shard_map/step/pallas_call | solution.py:502
  54.2 0.6 %copy.9 = f32[3,4096]{1,0:T(4,128)} copy(f32[3,4096]{1,0:T(4,128)S(1)} %step.1) | data formatting | bytes 98304
